TPU v7x, 32 devices: a whole 2x2x4 slice. The times are simulated.
32 devices in a mesh: coarse: 8 (over y, x, core), fine: 4 (over z).
Axes of the slice: x: 2, y: 2, z: 4, core: 2. Of those that a mesh axis runs over, the one named last changes fastest.
Arguments:
- activations: bfloat16 [16384, 1280], P(('coarse', 'fine')), may hold values from -6 to 6
- targets: int32 [16384], P(('coarse', 'fine')), may hold values from 0 to 4
- inner_squeeze_weight: bfloat16 [1280, 640], replicated, may hold values from -0.15625 to 0.15625
- inner_filter_taps: bfloat16 [3, 640, 640], replicated, may hold values from -0.125 to 0.125
- inner_expand_weight: bfloat16 [640, 1280], replicated, may hold values from -0.25 to 0.25
- outer_squeeze_weight: bfloat16 [1280, 640], replicated, may hold values from -0.15625 to 0.15625
- outer_filter_taps: bfloat16 [3, 640, 640], replicated, may hold values from -0.125 to 0.125
- outer_expand_weight: bfloat16 [640, 1280], replicated, may hold values from -0.25 to 0.25
- decoder: bfloat16 [5, 1280], replicated, may hold values from -0.059814453 to 0.059814453
Outputs:
- input_gradient: bfloat16 [16384, 1280], P(('coarse', 'fine'))
- token_loss: float32 [16384], P(('coarse', 'fine'))
All inputs are finite; a program needn't handle non-finite values.
Results may differ from a plain program's by a relative error of at most 0.015.
Values may be sent and summed in bfloat16 or wider, within the bound.
No kernel may reach another device: no remote copies, remote signals or barrier semaphores. Data moves between devices by JAX's collectives and lax.ppermute only.
A program may use at most 64 MiB of HBM per device.

v0:
```python
import math

import jax
import jax.numpy as jnp
from jax import lax
from jax.sharding import PartitionSpec as P

COARSE_HOP = 4


eps = 1e-05


def from_behind(value, axis, steps):
    count = lax.axis_size(axis)
    pairs = [(source, (source + steps) % count) for source in range(count)]
    return lax.ppermute(value, axis, pairs)


def norm_rows(values):
    average = jnp.mean(values, axis=-1, keepdims=True)
    centred = values - average
    factor = lax.rsqrt(jnp.mean(centred * centred, axis=-1, keepdims=True) + eps)
    return (centred * factor, factor)


def norm_back(normal, factor, upward):
    first_term = upward - jnp.mean(upward, axis=-1, keepdims=True)
    return (first_term - normal * jnp.mean(upward * normal, axis=-1, keepdims=True)) * factor


def gelu_exact(inputs):
    return 0.5 * inputs * (1.0 + lax.erf(inputs * (1.0 / math.sqrt(2.0))))


def gelu_slope(inputs):
    return 0.5 * (1.0 + lax.erf(inputs * (1.0 / math.sqrt(2.0)))) + inputs * jnp.exp(
        -0.5 * inputs * inputs
    ) * (1.0 / math.sqrt(2.0 * math.pi))


def product(leading, trailing):
    return jnp.dot(leading, trailing, preferred_element_type=jnp.float32)


def product_t(leading, trailing):
    return lax.dot_general(
        leading, trailing, (((1,), (1,)), ((), ())), preferred_element_type=jnp.float32
    )


def inner_pair(shard_rows):
    near_behind = from_behind(shard_rows, "fine", 2)
    near_ahead = from_behind(shard_rows, "fine", -2)
    far_behind = from_behind(near_behind, "coarse", 1)
    far_ahead = from_behind(near_ahead, "coarse", -1)
    fine_index = lax.axis_index("fine")
    fine_count = lax.axis_size("fine")
    behind_rows = jnp.where(fine_index < 2, far_behind, near_behind)
    ahead_rows = jnp.where(fine_index >= fine_count - 2, far_ahead, near_ahead)
    return (behind_rows, ahead_rows)


def outer_pair(shard_rows):
    behind_rows = from_behind(shard_rows, "coarse", COARSE_HOP)
    ahead_rows = from_behind(shard_rows, "coarse", -COARSE_HOP)
    return (behind_rows, ahead_rows)


def residual_block_forward(block_in, squeeze, taps, expand, neighbours):
    normal_in, _ = norm_rows(block_in.astype(jnp.float32))
    entry_act = gelu_exact(normal_in).astype(jnp.bfloat16)
    squeezed = product(entry_act, squeeze)
    normal_mid, _ = norm_rows(squeezed)
    middle = gelu_exact(normal_mid).astype(jnp.bfloat16)
    behind_rows, ahead_rows = neighbours(middle)
    conv_sum = (
        product(behind_rows, taps[0]) + product(middle, taps[1]) + product(ahead_rows, taps[2])
    )
    normal_conv, _ = norm_rows(conv_sum)
    closing = gelu_exact(normal_conv).astype(jnp.bfloat16)
    block_out = (block_in.astype(jnp.float32) + product(closing, expand)).astype(jnp.bfloat16)
    return (block_out, squeezed, conv_sum)


def residual_block_backward(
    block_in, squeezed, conv_sum, squeeze, taps, expand, neighbours, gradient_result
):
    dclosing = product_t(gradient_result.astype(jnp.bfloat16), expand)
    normal_conv, factor_conv = norm_rows(conv_sum)
    dconv = norm_back(normal_conv, factor_conv, gelu_slope(normal_conv) * dclosing).astype(
        jnp.bfloat16
    )
    behind_rows, ahead_rows = neighbours(dconv)
    dmiddle = (
        product_t(ahead_rows, taps[0]) + product_t(dconv, taps[1]) + product_t(behind_rows, taps[2])
    )
    normal_mid, factor_mid = norm_rows(squeezed)
    dsqueezed = norm_back(normal_mid, factor_mid, gelu_slope(normal_mid) * dmiddle).astype(
        jnp.bfloat16
    )
    dentry = product_t(dsqueezed, squeeze)
    normal_in, factor_in = norm_rows(block_in.astype(jnp.float32))
    return gradient_result + norm_back(normal_in, factor_in, gelu_slope(normal_in) * dentry)


def on_device(
    activations,
    targets,
    inner_squeeze_weight,
    inner_filter_taps,
    inner_expand_weight,
    outer_squeeze_weight,
    outer_filter_taps,
    outer_expand_weight,
    decoder,
):
    outer_block_input, inner_bottleneck_rows, inner_convolved = residual_block_forward(
        activations, inner_squeeze_weight, inner_filter_taps, inner_expand_weight, inner_pair
    )
    final_output, outer_bottleneck_rows, outer_convolved = residual_block_forward(
        outer_block_input, outer_squeeze_weight, outer_filter_taps, outer_expand_weight, outer_pair
    )
    normal_final, factor_final = norm_rows(final_output.astype(jnp.float32))
    normed = normal_final.astype(jnp.bfloat16)
    logits = product_t(normed, decoder)
    exponent = jnp.exp(logits)
    totals = jnp.sum(exponent, axis=-1, keepdims=True)
    classes = jnp.arange(decoder.shape[0], dtype=jnp.int32)
    onehot = (targets[:, None] == classes[None, :]).astype(jnp.float32)
    token_loss = jnp.log(totals[:, 0]) - jnp.sum(logits * onehot, axis=-1)
    dlogits = (32.0 * (exponent / totals - onehot)).astype(jnp.bfloat16)
    gradient_result = norm_back(normal_final, factor_final, product(dlogits, decoder))
    gradient_result = residual_block_backward(
        outer_block_input,
        outer_bottleneck_rows,
        outer_convolved,
        outer_squeeze_weight,
        outer_filter_taps,
        outer_expand_weight,
        outer_pair,
        gradient_result,
    )
    gradient_result = residual_block_backward(
        activations,
        inner_bottleneck_rows,
        inner_convolved,
        inner_squeeze_weight,
        inner_filter_taps,
        inner_expand_weight,
        inner_pair,
        gradient_result,
    )
    return (gradient_result.astype(jnp.bfloat16), token_loss)


def solution(mesh):
    in_specs = (
        P(("coarse", "fine"), None),
        P(("coarse", "fine")),
        P(),
        P(),
        P(),
        P(),
        P(),
        P(),
        P(),
    )
    out_specs = (P(("coarse", "fine"), None), P(("coarse", "fine")))
    return jax.shard_map(
        on_device, mesh=mesh, in_specs=in_specs, out_specs=out_specs, check_vma=False
    )
```

profile of v0, /device:TPU:1, one launch (start us, length us, event | category | flops | bytes accessed | tf_op | source)
XLA Modules:
  0.0 168.8 jit_solution(13413966147586752110)
XLA Ops:
  0.7 1.7 %convert_reduce_fusion.1 = f32[512]{0:T(512)S(1)} fusion(bf16[512,1280]{1,0:T(8,128)(2,1)} %param.9), kind=kLoop, calls=%fused_computation.7 | loop fusion | flops 1310208 | bytes 1312768 | tf_op jit(solution)/shard_map/reduce_sum | solution.py:21
  2.5 0.5 fusion.43
  3.0 3.1 %fusion.161 = (f32[512]{0:T(512)S(1)}, f32[512,640]{1,0:T(8,128)S(1)}) fusion(bf16[1280,640]{1,0:T(8,128)(2,1)} %param.11, bf16[512,1280]{1,0:T(8,128)(2,1)S(1)} %copy-done.1, f32[512]{0:T(512)S(1)} %add_rsqrt_fusion.6, f32[512]{0:T(512)S(1)} %broadcast_multiply_fusion.20), kind=kOutput, calls=%fused_computation.234 | convolution fusion | flops 844430848 | bytes 4265984 | tf_op jit(solution)/shard_map/dot_general | solution.py:43
  6.4 0.4 multiply_convert_fusion.7
  6.8 0.3 copy-done.4
  7.2 3.1 %collective-permute-start = (bf16[512,640]{1,0:T(8,128)(2,1)S(1)}, bf16[512,640]{1,0:T(8,128)(2,1)}, u32[]{:S(2)}, u32[]{:S(2)}) collective-permute-start(bf16[512,640]{1,0:T(8,128)(2,1)S(1)} %multiply_convert_fusion.7), channel_id=1, source_target_pairs={{0,2},{1,3},{2,0},{3,1},{4,6},{5,7},{6,4},{7,5},{8,10},{9,11},{10,... | collective-permute-start | bytes 1966088 | tf_op jit(solution)/shard_map/ppermute | solution.py:17
  10.3 28.6 %collective-permute-done = bf16[512,640]{1,0:T(8,128)(2,1)} collective-permute-done((bf16[512,640]{1,0:T(8,128)(2,1)S(1)}, bf16[512,640]{1,0:T(8,128)(2,1)}, u32[]{:S(2)}, u32[]{:S(2)}) %collective-permute-start) | collective-permute-done | bytes 655392 | tf_op jit(solution)/shard_map/ppermute | solution.py:17
  38.9 1.3 collective-permute-start.2
  40.1 1.2 collective-permute-start.1
  41.3 2.2 %fusion.104 = f32[512,640]{1,0:T(8,128)S(1)} fusion(bf16[512,640]{1,0:T(8,128)(2,1)} %copy-done.6, bf16[3,640,640]{2,1,0:T(8,128)(2,1)} %param.12), kind=kOutput, calls=%fused_computation.147 | convolution fusion | flops 419430400 | bytes 2785280 | tf_op jit(solution)/shard_map/dot_general | solution.py:43
  43.5 12.7 %collective-permute-done.2 = bf16[512,640]{1,0:T(8,128)(2,1)} collective-permute-done((bf16[512,640]{1,0:T(8,128)(2,1)}, bf16[512,640]{1,0:T(8,128)(2,1)}, u32[]{:S(2)}, u32[]{:S(2)}) %collective-permute-start.2) | collective-permute-done | bytes 655392 | tf_op jit(solution)/shard_map/ppermute | solution.py:17
  56.2 1.9 %fusion.100 = f32[512,640]{1,0:T(8,128)S(1)} fusion(bf16[3,640,640]{2,1,0:T(8,128)(2,1)S(1)} %copy-done.3, bf16[512,640]{1,0:T(8,128)(2,1)} %collective-permute-done.2, bf16[512,640]{1,0:T(8,128)(2,1)} %collective-permute-done, pred[]{:T(512)S(6)} %ge.4), kind=kOutput, calls=%fused_computation.143 | convolution fusion | flops 419758080 | bytes 3440641 | tf_op jit(solution)/shard_map/dot_general | solution.py:43
  58.2 2.1 %fusion.162 = (f32[512]{0:T(512)S(1)}, f32[512,640]{1,0:T(8,128)S(1)}) fusion(f32[512,640]{1,0:T(8,128)S(1)} %fusion.100, f32[512,640]{1,0:T(8,128)S(1)} %fusion.104, bf16[3,640,640]{2,1,0:T(8,128)(2,1)S(1)} %copy-done.3, bf16[512,640]{1,0:T(8,128)(2,1)} %collective-permute-done.1, bf16[512,640]{1,0:T(8,128)(2,1)} %collective-permute-done, pred[]{:T(512)S(6)} %lt.4), kind=kOutput, calls=%fused_computation.235 | convolution fusion | flops 420740608 | bytes 6064129 | tf_op jit(solution)/shard_map/dot_general | solution.py:43
  60.3 0.3 multiply_reduce_fusion.6
  60.7 1.5 convert_reduce_fusion
  62.1 0.5 fusion.31
  62.6 1.7 %fusion.163 = (f32[512]{0:T(512)S(1)}, f32[512,640]{1,0:T(8,128)S(1)}) fusion(bf16[1280,640]{1,0:T(8,128)(2,1)S(1)} %copy-done.9, bf16[512,1280]{1,0:T(8,128)(2,1)S(1)} %get-tuple-element.23, f32[512]{0:T(512)S(1)} %add_rsqrt_fusion.3, f32[512]{0:T(512)S(1)} %broadcast_multiply_fusion.19), kind=kOutput, calls=%fused_computation.236 | convolution fusion | flops 844430848 | bytes 4265984 | tf_op jit(solution)/shard_map/dot_general | solution.py:43
  64.7 0.4 multiply_convert_fusion.5
  65.1 1.3 collective-permute-start.3
  66.4 0.7 fusion.94
  67.2 13.9 %collective-permute-done.3 = bf16[512,640]{1,0:T(8,128)(2,1)S(1)} collective-permute-done((bf16[512,640]{1,0:T(8,128)(2,1)S(1)}, bf16[512,640]{1,0:T(8,128)(2,1)S(1)}, u32[]{:S(2)}, u32[]{:S(2)}) %collective-permute-start.3) | collective-permute-done | bytes 655392 | tf_op jit(solution)/shard_map/ppermute | solution.py:17
  81.1 0.7 fusion.90
  81.8 0.9 fusion.164
  82.7 0.3 multiply_reduce_fusion.4
  83.0 1.5 convert_reduce_fusion.2
  84.5 0.5 fusion.47
  85.2 0.6 select_reduce_fusion
  85.9 1.0 fusion.156
  86.9 2.3 %fusion.160 = (f32[512]{0:T(512)S(1)}, f32[512]{0:T(512)S(1)}, f32[512,640]{1,0:T(8,128)S(1)}) fusion(f32[512]{0:T(512)S(1)} %add_rsqrt_fusion.1, f32[512,640]{1,0:T(8,128)S(1)} %get-tuple-element.27, f32[512]{0:T(512)S(1)} %broadcast_multiply_fusion.8, bf16[640,1280]{1,0:T(8,128)(2,1)S(1)} %copy-done, f32[512]{0:T(512)S(1)} %get-tuple-element.38, ...), kind=kOutput, calls=%fused_computation.233 | convolution fusion | flops 848690176 | bytes 8208384 | tf_op jit(solution)/shard_map/dot_general | solution.py:47
  89.3 0.4 multiply_convert_fusion.3
  89.6 1.8 %collective-permute-start.4 = (bf16[512,640]{1,0:T(8,128)(2,1)S(1)}, bf16[512,640]{1,0:T(8,128)(2,1)S(1)}, u32[]{:S(2)}, u32[]{:S(2)}) collective-permute-start(bf16[512,640]{1,0:T(8,128)(2,1)S(1)} %multiply_convert_fusion.3), channel_id=1, source_target_pairs={{0,16},{4,20},{8,24},{12,28},{16,0},{20,4},{24,8},{28,12},{1,17},{... | collective-permute-start | bytes 1966088 | tf_op jit(solution)/shard_map/ppermute | solution.py:17
  91.4 0.8 fusion.92
  92.2 13.0 %collective-permute-done.4 = bf16[512,640]{1,0:T(8,128)(2,1)S(1)} collective-permute-done((bf16[512,640]{1,0:T(8,128)(2,1)S(1)}, bf16[512,640]{1,0:T(8,128)(2,1)S(1)}, u32[]{:S(2)}, u32[]{:S(2)}) %collective-permute-start.4) | collective-permute-done | bytes 655392 | tf_op jit(solution)/shard_map/ppermute | solution.py:17
  105.2 0.8 fusion.88
  106.0 1.5 fusion.159
  107.5 2.4 %fusion.155 = (f32[512]{0:T(512)S(1)}, f32[512]{0:T(512)S(1)}, f32[512,1280]{1,0:T(8,128)S(1)}) fusion(f32[512]{0:T(512)S(1)} %add_rsqrt_fusion.3, f32[512]{0:T(512)S(1)} %broadcast_multiply_fusion.19, bf16[512,1280]{1,0:T(8,128)(2,1)S(1)} %get-tuple-element.23, bf16[1280,640]{1,0:T(8,128)(2,1)S(1)} %copy-done.9, f32[512,640]{1,0:T(8,128)S(1)} %get-tuple-element.33, ...), kind=kOutput, calls=%fused_computation.228 | convolution fusion | flops 850983936 | bytes 8208384 | tf_op jit(solution)/shard_map/dot_general | solution.py:47
  109.9 1.7 fusion.27
  111.6 1.7 %fusion.158 = (f32[512]{0:T(512)S(1)}, f32[512]{0:T(512)S(1)}, f32[512,640]{1,0:T(8,128)S(1)}) fusion(f32[512]{0:T(512)S(1)} %add_rsqrt_fusion.4, f32[512,640]{1,0:T(8,128)S(1)} %get-tuple-element.21, f32[512]{0:T(512)S(1)} %broadcast_multiply_fusion.10, bf16[640,1280]{1,0:T(8,128)(2,1)S(1)} %copy-done.10, f32[512,1280]{1,0:T(8,128)S(1)} %fusion.27), kind=kOutput, calls=%fused_computation.231 | convolution fusion | flops 844102656 | bytes 6889472 | tf_op jit(solution)/shard_map/dot_general | solution.py:47
  113.3 0.4 multiply_convert_fusion.1
  113.8 29.6 %collective-permute-done.5 = bf16[512,640]{1,0:T(8,128)(2,1)S(1)} collective-permute-done((bf16[512,640]{1,0:T(8,128)(2,1)S(1)}, bf16[512,640]{1,0:T(8,128)(2,1)S(1)}, u32[]{:S(2)}, u32[]{:S(2)}) %collective-permute-start.5) | collective-permute-done | bytes 655392 | tf_op jit(solution)/shard_map/ppermute | solution.py:17
  143.4 4.5 %collective-permute-start.7 = (bf16[512,640]{1,0:T(8,128)(2,1)S(1)}, bf16[512,640]{1,0:T(8,128)(2,1)S(1)}, u32[]{:S(2)}, u32[]{:S(2)}) collective-permute-start(bf16[512,640]{1,0:T(8,128)(2,1)S(1)} %collective-permute-done.5), channel_id=1, source_target_pairs={{0,4},{4,8},{8,12},{12,16},{16,20},{20,24},{24,28},{28,0},{1,5},{5... | collective-permute-start | bytes 1966088 | tf_op jit(solution)/shard_map/ppermute | solution.py:17
  147.9 0.6 log_subtract_fusion
  148.5 0.8 fusion.102
  149.3 12.8 %collective-permute-done.7 = bf16[512,640]{1,0:T(8,128)(2,1)S(1)} collective-permute-done((bf16[512,640]{1,0:T(8,128)(2,1)S(1)}, bf16[512,640]{1,0:T(8,128)(2,1)S(1)}, u32[]{:S(2)}, u32[]{:S(2)}) %collective-permute-start.7) | collective-permute-done | bytes 655392 | tf_op jit(solution)/shard_map/ppermute | solution.py:17
  162.1 0.8 fusion.98
  162.9 1.5 fusion.157
  164.5 2.4 %fusion.154 = (f32[512]{0:T(512)S(1)}, f32[512]{0:T(512)S(1)}, f32[512,1280]{1,0:T(8,128)S(1)}) fusion(f32[512]{0:T(512)S(1)} %add_rsqrt_fusion.6, f32[512]{0:T(512)S(1)} %broadcast_multiply_fusion.20, bf16[512,1280]{1,0:T(8,128)(2,1)S(1)} %copy-done.1, bf16[1280,640]{1,0:T(8,128)(2,1)S(1)} %copy-done.11, f32[512,640]{1,0:T(8,128)S(1)} %get-tuple-element.36, ...), kind=kOutput, calls=%fused_computation.227 | convolution fusion | flops 850983936 | bytes 8208384 | tf_op jit(solution)/shard_map/dot_general | solution.py:47
  166.9 1.9 %fusion.39 = bf16[512,1280]{1,0:T(8,128)(2,1)} fusion(f32[512,1280]{1,0:T(8,128)S(1)} %fusion.27, bf16[512,1280]{1,0:T(8,128)(2,1)S(1)} %copy-done.1, f32[512,1280]{1,0:T(8,128)S(1)} %get-tuple-element.37, f32[512]{0:T(512)S(1)} %broadcast_multiply_fusion.12, f32[512]{0:T(512)S(1)} %broadcast_multiply_fusion.13, f32[512]{0:T(512)S(1)} %add_rsqrt_fusion.6, ...), kind=kLoop, calls=%fused_computation.51 | loop fusion | flops 5898240 | bytes 7872512 | tf_op jit(solution)/shard_map/convert_element_type | solution.py:154
  (56 shorter events, 1.2 us)
Async XLA Ops:
  0.6 82.4 %copy-start = (bf16[640,1280]{1,0:T(8,128)(2,1)S(1)}, bf16[640,1280]{1,0:T(8,128)(2,1)}, u32[]{:S(2)}) copy-start(bf16[640,1280]{1,0:T(8,128)(2,1)} %param.16) | copy-start | bytes 4915204
  0.6 1.8 %copy-start.1 = (bf16[512,1280]{1,0:T(8,128)(2,1)S(1)}, bf16[512,1280]{1,0:T(8,128)(2,1)}, u32[]{:S(2)}) copy-start(bf16[512,1280]{1,0:T(8,128)(2,1)} %param.9) | copy-start | bytes 3932164
  6.1 1.1 copy-start.4
  7.2 3.1 %copy-start.6 = (bf16[512,640]{1,0:T(8,128)(2,1)}, bf16[512,640]{1,0:T(8,128)(2,1)S(1)}, u32[]{:S(2)}) copy-start(bf16[512,640]{1,0:T(8,128)(2,1)S(1)} %multiply_convert_fusion.7) | copy-start | bytes 1966084
  7.2 31.7 %collective-permute-start = (bf16[512,640]{1,0:T(8,128)(2,1)S(1)}, bf16[512,640]{1,0:T(8,128)(2,1)}, u32[]{:S(2)}, u32[]{:S(2)}) collective-permute-start(bf16[512,640]{1,0:T(8,128)(2,1)S(1)} %multiply_convert_fusion.7), channel_id=1, source_target_pairs={{0,2},{1,3},{2,0},{3,1},{4,6},{5,7},{6,4},{7,5},{8,10},{9,11},{10,... | collective-permute-start | bytes 1966088 | tf_op jit(solution)/shard_map/ppermute | solution.py:17
  38.9 17.4 %collective-permute-start.2 = (bf16[512,640]{1,0:T(8,128)(2,1)}, bf16[512,640]{1,0:T(8,128)(2,1)}, u32[]{:S(2)}, u32[]{:S(2)}) collective-permute-start(bf16[512,640]{1,0:T(8,128)(2,1)} %collective-permute-done), channel_id=1, source_target_pairs={{0,28},{4,0},{8,4},{12,8},{16,12},{20,16},{24,20},{28,24},{1,29},{... | collective-permute-start | bytes 1966088 | tf_op jit(solution)/shard_map/ppermute | solution.py:17
  40.1 18.0 %collective-permute-start.1 = (bf16[512,640]{1,0:T(8,128)(2,1)}, bf16[512,640]{1,0:T(8,128)(2,1)}, u32[]{:S(2)}, u32[]{:S(2)}) collective-permute-start(bf16[512,640]{1,0:T(8,128)(2,1)} %collective-permute-done), channel_id=1, source_target_pairs={{0,4},{4,8},{8,12},{12,16},{16,20},{20,24},{24,28},{28,0},{1,5},{5... | collective-permute-start | bytes 1966088 | tf_op jit(solution)/shard_map/ppermute | solution.py:17
  41.3 14.9 %copy-start.3 = (bf16[3,640,640]{2,1,0:T(8,128)(2,1)S(1)}, bf16[3,640,640]{2,1,0:T(8,128)(2,1)}, u32[]{:S(2)}) copy-start(bf16[3,640,640]{2,1,0:T(8,128)(2,1)} %param.12) | copy-start | bytes 7372804
  58.2 2.5 %copy-start.10 = (bf16[640,1280]{1,0:T(8,128)(2,1)S(1)}, bf16[640,1280]{1,0:T(8,128)(2,1)}, u32[]{:S(2)}) copy-start(bf16[640,1280]{1,0:T(8,128)(2,1)} %param.13) | copy-start | bytes 4915204
  60.6 2.0 %copy-start.9 = (bf16[1280,640]{1,0:T(8,128)(2,1)S(1)}, bf16[1280,640]{1,0:T(8,128)(2,1)}, u32[]{:S(2)}) copy-start(bf16[1280,640]{1,0:T(8,128)(2,1)} %param.14) | copy-start | bytes 4915204
  64.4 2.0 %copy-start.2 = (bf16[3,640,640]{2,1,0:T(8,128)(2,1)S(1)}, bf16[3,640,640]{2,1,0:T(8,128)(2,1)}, u32[]{:S(2)}) copy-start(bf16[3,640,640]{2,1,0:T(8,128)(2,1)} %param.15) | copy-start | bytes 7372804
  65.1 16.0 %collective-permute-start.3 = (bf16[512,640]{1,0:T(8,128)(2,1)S(1)}, bf16[512,640]{1,0:T(8,128)(2,1)S(1)}, u32[]{:S(2)}, u32[]{:S(2)}) collective-permute-start(bf16[512,640]{1,0:T(8,128)(2,1)S(1)} %multiply_convert_fusion.5), channel_id=1, source_target_pairs={{0,16},{4,20},{8,24},{12,28},{16,0},{20,4},{24,8},{28,12},{1,17},{... | collective-permute-start | bytes 1966088 | tf_op jit(solution)/shard_map/ppermute | solution.py:17
  84.5 0.7 copy-start.7
  84.5 0.7 copy-start.8
  89.6 15.6 %collective-permute-start.4 = (bf16[512,640]{1,0:T(8,128)(2,1)S(1)}, bf16[512,640]{1,0:T(8,128)(2,1)S(1)}, u32[]{:S(2)}, u32[]{:S(2)}) collective-permute-start(bf16[512,640]{1,0:T(8,128)(2,1)S(1)} %multiply_convert_fusion.3), channel_id=1, source_target_pairs={{0,16},{4,20},{8,24},{12,28},{16,0},{20,4},{24,8},{28,12},{1,17},{... | collective-permute-start | bytes 1966088 | tf_op jit(solution)/shard_map/ppermute | solution.py:17
  113.7 29.7 %collective-permute-start.5 = (bf16[512,640]{1,0:T(8,128)(2,1)S(1)}, bf16[512,640]{1,0:T(8,128)(2,1)S(1)}, u32[]{:S(2)}, u32[]{:S(2)}) collective-permute-start(bf16[512,640]{1,0:T(8,128)(2,1)S(1)} %multiply_convert_fusion.1), channel_id=1, source_target_pairs={{0,2},{1,3},{2,0},{3,1},{4,6},{5,7},{6,4},{7,5},{8,10},{9,11},{10,... | collective-permute-start | bytes 1966088 | tf_op jit(solution)/shard_map/ppermute | solution.py:17
  143.4 18.7 %collective-permute-start.7 = (bf16[512,640]{1,0:T(8,128)(2,1)S(1)}, bf16[512,640]{1,0:T(8,128)(2,1)S(1)}, u32[]{:S(2)}, u32[]{:S(2)}) collective-permute-start(bf16[512,640]{1,0:T(8,128)(2,1)S(1)} %collective-permute-done.5), channel_id=1, source_target_pairs={{0,4},{4,8},{8,12},{12,16},{16,20},{20,24},{24,28},{28,0},{1,5},{5... | collective-permute-start | bytes 1966088 | tf_op jit(solution)/shard_map/ppermute | solution.py:17
  147.9 15.0 %collective-permute-start.6 = (bf16[512,640]{1,0:T(8,128)(2,1)S(1)}, bf16[512,640]{1,0:T(8,128)(2,1)S(1)}, u32[]{:S(2)}, u32[]{:S(2)}) collective-permute-start(bf16[512,640]{1,0:T(8,128)(2,1)S(1)} %collective-permute-done.5), channel_id=1, source_target_pairs={{0,28},{4,0},{8,4},{12,8},{16,12},{20,16},{24,20},{28,24},{1,29},{... | collective-permute-start | bytes 1966088 | tf_op jit(solution)/shard_map/ppermute | solution.py:17
  149.3 13.6 %copy-start.5 = (f32[512,640]{1,0:T(8,128)S(1)}, f32[512,640]{1,0:T(8,128)}, u32[]{:S(2)}) copy-start(f32[512,640]{1,0:T(8,128)} %copy-done.4) | copy-start | bytes 3932164
  162.9 1.5 copy-start.11
where the time goes:
time: 169 us
  waiting for transfers between devices  111 us (66%)
  matrix products  33.1 us (20%)
  starting transfers between devices  13.2 us (8%)
  other arithmetic  10.2 us (6%)
    ppermute x8, waiting for transfers between devices, from_behind(): return lax.ppermute(value, axis, pairs)  111 us
    dot_general x11, matrix products, product(): return jnp.dot(leading, trailing, preferred_element_type=jnp.float32)  17.5 us
    dot_general x11, matrix products, product_t(): lax.dot_general(leading, trailing, (((1,), (1,)), ((), ())), preferred_el...  15.6 us
    ppermute x8, starting transfers between devices, from_behind(): return lax.ppermute(value, axis, pairs)  13.2 us
  transfers between devices with their start and end apart: 8, of which 6 were waited for; matrix products, arithmetic and copies ran while one was open for 5% of the time, Pallas kernels for 0%

commit v1 on v0

--- a/solution.py
+++ b/solution.py
@@ -1,11 +1,18 @@
+import functools
 import math
 
 import jax
 import jax.numpy as jnp
 from jax import lax
+from jax.experimental import pallas as pl
+from jax.experimental.pallas import tpu as pltpu
 from jax.sharding import PartitionSpec as P
 
 COARSE_HOP = 4
+FINE_HOP = 2
+LANES = 128
+CHUNKS = 1
+BLOCK = 128
 
 
 eps = 1e-05
@@ -154,6 +161,220 @@
     return (gradient_result.astype(jnp.bfloat16), token_loss)
 
 
+BF = jnp.bfloat16
+F32 = jnp.float32
+
+
+def activate(values, normal_ref, slope_ref, factor_ref, rows):
+    normal, factor = norm_rows(values)
+    half = 0.5 * (1.0 + lax.erf(normal * (1.0 / math.sqrt(2.0))))
+    bell = jnp.exp(-0.5 * normal * normal) * (1.0 / math.sqrt(2.0 * math.pi))
+    normal_ref[rows, :] = normal
+    slope_ref[rows, :] = half + normal * bell
+    factor_ref[rows, :] = jnp.broadcast_to(factor, (factor.shape[0], LANES))
+    return (normal * half).astype(BF)
+
+
+def back(upward, normal_ref, slope_ref, factor_ref, rows):
+    factor = factor_ref[rows, :][:, :1]
+    return norm_back(normal_ref[rows, :], factor, slope_ref[rows, :] * upward)
+
+
+def chain_kernel(
+    near, far, classes, block,
+    x_ref, onehot_ref, ws_in, wt_in, we_in, ws_out, wt_out, we_out, dec_ref,
+    grad_ref, loss_ref,
+    mid_a, mid_b, outer_in, carried,
+    n_in_a, s_in_a, f_in_a, n_mid_a, s_mid_a, f_mid_a, n_con_a, s_con_a, f_con_a,
+    n_in_b, s_in_b, f_in_b, n_mid_b, s_mid_b, f_mid_b, n_con_b, s_con_b, f_con_b,
+):
+    total = x_ref.shape[0]
+    steps = total // block
+
+    def each(body):
+        def run(step, carry):
+            body(pl.multiple_of(step * block, block))
+            return carry
+
+        lax.fori_loop(0, steps, run, 0)
+
+    def wrap(ref):
+        ref[pl.ds(0, near), :] = ref[pl.ds(total, near), :]
+        ref[pl.ds(total + near, near), :] = ref[pl.ds(near, near), :]
+
+    def near_rows(ref, start, shift):
+        return ref[pl.ds(pl.multiple_of(start + near + shift, near), block), :]
+
+    def far_rows(ref, start, shift):
+        return ref[pl.ds(pl.multiple_of(lax.rem(start + shift, total), block), block), :]
+
+    def enter(start):
+        rows = pl.ds(start, block)
+        entry = activate(x_ref[rows, :].astype(F32), n_in_a, s_in_a, f_in_a, rows)
+        squeezed = product(entry, ws_in[...])
+        middle = activate(squeezed, n_mid_a, s_mid_a, f_mid_a, rows)
+        mid_a[pl.ds(pl.multiple_of(start + near, near), block), :] = middle
+
+    each(enter)
+    wrap(mid_a)
+
+    def inner(start):
+        rows = pl.ds(start, block)
+        conv = (
+            product(near_rows(mid_a, start, -near), wt_in[0])
+            + product(near_rows(mid_a, start, 0), wt_in[1])
+            + product(near_rows(mid_a, start, near), wt_in[2])
+        )
+        closing = activate(conv, n_con_a, s_con_a, f_con_a, rows)
+        following = (x_ref[rows, :].astype(F32) + product(closing, we_in[...])).astype(BF)
+        outer_in[rows, :] = following
+        entry = activate(following.astype(F32), n_in_b, s_in_b, f_in_b, rows)
+        squeezed = product(entry, ws_out[...])
+        mid_b[rows, :] = activate(squeezed, n_mid_b, s_mid_b, f_mid_b, rows)
+
+    each(inner)
+
+    def outer(start):
+        rows = pl.ds(start, block)
+        conv = (
+            product(far_rows(mid_b, start, total - far), wt_out[0])
+            + product(mid_b[rows, :], wt_out[1])
+            + product(far_rows(mid_b, start, far), wt_out[2])
+        )
+        closing = activate(conv, n_con_b, s_con_b, f_con_b, rows)
+        final = (outer_in[rows, :].astype(F32) + product(closing, we_out[...])).astype(BF)
+        normal, factor = norm_rows(final.astype(F32))
+        logits = product_t(normal.astype(BF), dec_ref[...])
+        lane = lax.broadcasted_iota(jnp.int32, logits.shape, 1)
+        exponent = jnp.where(lane < classes, jnp.exp(logits), 0.0)
+        totals = jnp.sum(exponent, axis=-1, keepdims=True)
+        onehot = onehot_ref[rows, :].astype(F32)
+        loss = jnp.log(totals) - jnp.sum(logits * onehot, axis=-1, keepdims=True)
+        loss = jnp.broadcast_to(loss, (block, LANES))
+        for part in range(block // LANES):
+            flat = jnp.transpose(loss[part * LANES : (part + 1) * LANES, :])
+            loss_ref[pl.ds(start // LANES + part, 1), :] = flat[:1, :]
+        dlogits = (32.0 * (exponent / totals - onehot)).astype(BF)
+        upward = norm_back(normal, factor, product(dlogits, dec_ref[...]))
+        carried[rows, :] = upward
+        dclosing = product_t(upward.astype(BF), we_out[...])
+        mid_a[rows, :] = back(dclosing, n_con_b, s_con_b, f_con_b, rows).astype(BF)
+
+    each(outer)
+
+    def outer_back(start):
+        rows = pl.ds(start, block)
+        dmiddle = (
+            product_t(far_rows(mid_a, start, far), wt_out[0])
+            + product_t(mid_a[rows, :], wt_out[1])
+            + product_t(far_rows(mid_a, start, total - far), wt_out[2])
+        )
+        dsqueezed = back(dmiddle, n_mid_b, s_mid_b, f_mid_b, rows).astype(BF)
+        dentry = product_t(dsqueezed, ws_out[...])
+        upward = carried[rows, :] + back(dentry, n_in_b, s_in_b, f_in_b, rows)
+        carried[rows, :] = upward
+        dclosing = product_t(upward.astype(BF), we_in[...])
+        mid_b[pl.ds(pl.multiple_of(start + near, near), block), :] = back(
+            dclosing, n_con_a, s_con_a, f_con_a, rows
+        ).astype(BF)
+
+    each(outer_back)
+    wrap(mid_b)
+
+    def inner_back(start):
+        rows = pl.ds(start, block)
+        dmiddle = (
+            product_t(near_rows(mid_b, start, near), wt_in[0])
+            + product_t(near_rows(mid_b, start, 0), wt_in[1])
+            + product_t(near_rows(mid_b, start, -near), wt_in[2])
+        )
+        dsqueezed = back(dmiddle, n_mid_a, s_mid_a, f_mid_a, rows).astype(BF)
+        dentry = product_t(dsqueezed, ws_in[...])
+        upward = carried[rows, :] + back(dentry, n_in_a, s_in_a, f_in_a, rows)
+        grad_ref[rows, :] = upward.astype(BF)
+
+    each(inner_back)
+
+
+def run_chains(rows, onehot, weights, near, far, classes, block):
+    count, width = rows.shape
+    bottleneck = weights[0].shape[1]
+    padded = count + 2 * near
+
+    def kept(size):
+        return [
+            pltpu.VMEM((count, size), F32),
+            pltpu.VMEM((count, size), F32),
+            pltpu.VMEM((count, LANES), F32),
+        ]
+
+    one_block = kept(width) + kept(bottleneck) + kept(bottleneck)
+    return pl.pallas_call(
+        functools.partial(chain_kernel, near, far, classes, block),
+        out_shape=(
+            jax.ShapeDtypeStruct((count, width), BF),
+            jax.ShapeDtypeStruct((count // LANES, LANES), F32),
+        ),
+        in_specs=[pl.BlockSpec(memory_space=pltpu.VMEM)] * (2 + len(weights)),
+        out_specs=(
+            pl.BlockSpec(memory_space=pltpu.VMEM),
+            pl.BlockSpec(memory_space=pltpu.VMEM),
+        ),
+        scratch_shapes=[
+            pltpu.VMEM((padded, bottleneck), BF),
+            pltpu.VMEM((padded, bottleneck), BF),
+            pltpu.VMEM((count, width), BF),
+            pltpu.VMEM((count, width), F32),
+        ]
+        + one_block
+        + one_block,
+        compiler_params=pltpu.CompilerParams(vmem_limit_bytes=60 * 1024 * 1024),
+        cost_estimate=pl.CostEstimate(
+            flops=count * 36 * width * bottleneck, bytes_accessed=24 << 20, transcendentals=0
+        ),
+    )(rows, onehot, *weights)
+
+
+def on_device_chains(chunks, block, activations, targets, *weights):
+    axes = ("coarse", "fine")
+    devices = lax.axis_size(axes)
+    rows, width = activations.shape
+    decoder = weights[-1]
+    classes = decoder.shape[0]
+    padded = jnp.pad(decoder, ((0, LANES - classes), (0, 0)))
+    weights = weights[:-1] + (padded,)
+    part = rows // chunks
+    each = part // devices
+    near = FINE_HOP * each
+    far = COARSE_HOP * lax.axis_size("fine") * each
+
+    def spread(values):
+        shaped = values.reshape((devices, each) + values.shape[1:])
+        moved = lax.all_to_all(shaped, axes, 0, 0, tiled=True)
+        return moved.reshape(values.shape)
+
+    grads, losses = [], []
+    lane = jnp.arange(LANES, dtype=jnp.int32)
+    for chunk in range(chunks):
+        piece = slice(chunk * part, (chunk + 1) * part)
+        there = spread(activations[piece])
+        onehot = (spread(targets[piece])[:, None] == lane[None, :]).astype(BF)
+        grad, loss = run_chains(there, onehot, weights, near, far, classes, block)
+        grads.append(spread(grad))
+        losses.append(spread(loss.reshape(part)))
+    return (jnp.concatenate(grads), jnp.concatenate(losses))
+
+
+def chains_fit(mesh, rows, chunks, block):
+    devices = mesh.shape["coarse"] * mesh.shape["fine"]
+    part = rows // chunks
+    if rows % chunks or part % devices or part % block or block % LANES:
+        return False
+    each = part // devices
+    far = COARSE_HOP * mesh.shape["fine"] * each
+    return (FINE_HOP * each) % 16 == 0 and block % (FINE_HOP * each) == 0 and far % block == 0
+
+
 def solution(mesh):
     in_specs = (
         P(("coarse", "fine"), None),
@@ -167,6 +388,14 @@
         P(),
     )
     out_specs = (P(("coarse", "fine"), None), P(("coarse", "fine")))
-    return jax.shard_map(
-        on_device, mesh=mesh, in_specs=in_specs, out_specs=out_specs, check_vma=False
-    )
+
+    def step(activations, *others):
+        rows = activations.shape[0] // mesh.size
+        body = on_device
+        if chains_fit(mesh, rows, CHUNKS, BLOCK):
+            body = functools.partial(on_device_chains, CHUNKS, BLOCK)
+        return jax.shard_map(
+            body, mesh=mesh, in_specs=in_specs, out_specs=out_specs, check_vma=False
+        )(activations, *others)
+
+    return step

time: 169 us -> 146 us (0.86)
  waiting for transfers between devices: 111 us -> 59.3 us
  Pallas kernels: 0 us -> 48.2 us
  matrix products: 33.1 us -> 0 us
  blocking collectives: 0 us -> 23.2 us
  other arithmetic: 10.2 us -> 2.16 us
  starting transfers between devices: 13.2 us -> 6.03 us
  local copies, waits for them, and re-layouts: 0.69 us -> 6.16 us
    ppermute x8 -> x0, waiting for transfers between devices: 111 us -> none  [from_behind(): return lax.ppermute(value, axis, pairs)]
    all_to_all x0 -> x2, waiting for transfers between devices: none -> 59.3 us  [spread(): moved = lax.all_to_all(shaped, axes, 0, 0, tiled=True)]
    pallas_call x0 -> x1, Pallas kernels: none -> 48.2 us  [run_chains(): pl.pallas_call(functools.partial(chain_kernel, near, far, classes, block)...]
    dot_general x22 -> x0, matrix products: 33.1 us -> none  [the longest x11 17.5 us: product(): return jnp.dot(leading, trailing, preferred_element_type=jnp.float32)]
    all_to_all x0 -> x2, blocking collectives: none -> 23.2 us  [spread(): moved = lax.all_to_all(shaped, axes, 0, 0, tiled=True)]
    ppermute x8 -> x0, starting transfers between devices: 13.2 us -> none  [from_behind(): return lax.ppermute(value, axis, pairs)]
    all_to_all x0 -> x2, starting transfers between devices: none -> 6.03 us  [spread(): moved = lax.all_to_all(shaped, axes, 0, 0, tiled=True)]
    reduce_sum x8 -> x0, other arithmetic: 4.34 us -> none  [the longest x7 2.63 us: norm_rows(): jnp.mean(centred * centred, axis=-1, keepdims=True) + eps]
  transfers between devices with their start and end apart: 8 -> 2, of which waited for: 6 -> 2; matrix products, arithmetic and copies ran while one was open for 5% -> 3% of each run, Pallas kernels for 0% -> 0%
where the time goes in v1:
time: 146 us
  waiting for transfers between devices  59.3 us (41%)
  Pallas kernels  48.2 us (33%)
  blocking collectives  23.2 us (16%)
  local copies, waits for them, and re-layouts  6.16 us (4%)
  starting transfers between devices  6.03 us (4%)
  other arithmetic  2.16 us (1%)
    all_to_all x2, waiting for transfers between devices, spread(): moved = lax.all_to_all(shaped, axes, 0, 0, tiled=True)  59.3 us
    pallas_call x1, Pallas kernels, run_chains(): pl.pallas_call(functools.partial(chain_kernel, near, far, classes, block)...  48.2 us
    all_to_all x2, blocking collectives, spread(): moved = lax.all_to_all(shaped, axes, 0, 0, tiled=True)  23.2 us
    all_to_all x2, starting transfers between devices, spread(): moved = lax.all_to_all(shaped, axes, 0, 0, tiled=True)  6.03 us
  transfers between devices with their start and end apart: 2, of which 2 were waited for; matrix products, arithmetic and copies ran while one was open for 3% of the time, Pallas kernels for 0%

profile of v1, /device:TPU:1, one launch (start us, length us, event | category | flops | bytes accessed | tf_op | source)
XLA Modules:
  0.0 145.7 jit_solution(2431681092743087546)
XLA Ops:
  0.6 0.0 copy-start.1
  0.6 0.8 all_to_all.19
  1.4 13.6 %all_to_all.28 = s32[32,1,16]{2,1,0:T(1,128)S(1)} all-to-all(s32[32,1,16]{2,1,0:T(1,128)S(1)} %bitcast.11), channel_id=1, replica_groups=mesh['coarse'=8,'fine'=4] {'coarse','fine'}, dimensions={0} | all-to-all | bytes 4096 | tf_op jit(solution)/shard_map/all_to_all | solution.py:353
  15.0 3.0 %all-to-all-start = ((bf16[32,16,1280]{2,1,0:T(8,128)(2,1)}), bf16[32,16,1280]{2,1,0:T(8,128)(2,1)S(1)}, u32[]{:S(2)}, u32[]{:S(2)}) async-start(bf16[32,16,1280]{2,1,0:T(8,128)(2,1)} %bitcast.7), calls=%async_computation | async-start | bytes 2621440 | tf_op jit(solution)/shard_map/all_to_all | solution.py:353
  18.0 0.0 copy-done.1
  18.0 0.8 pad.4.dec_ref
  18.8 0.5 broadcast.8
  19.3 0.7 reduce.6
  20.0 0.1 eq.15
  20.1 0.8 fusion.onehot_ref
  20.9 29.1 %all-to-all-done = bf16[32,16,1280]{2,1,0:T(8,128)(2,1)S(1)} async-done(((bf16[32,16,1280]{2,1,0:T(8,128)(2,1)}), bf16[32,16,1280]{2,1,0:T(8,128)(2,1)S(1)}, u32[]{:S(2)}, u32[]{:S(2)}) %all-to-all-start) | async-done | bytes 1310752 | tf_op jit(solution)/shard_map/all_to_all | solution.py:353
  50.0 0.0 copy-start
  50.0 1.1 copy-done
  51.1 48.2 %shard_map.104 = (bf16[512,1280]{1,0:T(8,128)(2,1)}, f32[4,128]{1,0:T(4,128)}) custom-call(bf16[512,1280]{1,0:T(8,128)(2,1)} %bitcast.8, bf16[512,128]{1,0:T(8,128)(2,1)} %fusion.onehot_ref, bf16[1280,640]{1,0:T(8,128)(2,1)} %ws_in.1, bf16[3,640,640]{2,1,0:T(8,128)(2,1)} %wt_in.1, bf16[640,1280]{1,0:T(8,128)(2,1)} %we_in.1, bf16[1280,640]{1,0:T(8,128)(2,1)} %ws_out.1, ...), custom_call_target="tpu_custom_call" | custom-call | flops 15099494400 | bytes 25165824 | tf_op jit(solution)/shard_map/pallas_call | solution.py:312
  99.2 0.8 all_to_all.22
  100.0 9.6 %all_to_all.29 = f32[32,1,16]{2,1,0:T(1,128)S(1)} all-to-all(f32[32,1,16]{2,1,0:T(1,128)S(1)} %bitcast.10), channel_id=1, replica_groups=mesh['coarse'=8,'fine'=4] {'coarse','fine'}, dimensions={0} | all-to-all | bytes 4096 | tf_op jit(solution)/shard_map/all_to_all | solution.py:353
  109.6 3.0 %all-to-all-start.2 = ((bf16[32,16,1280]{2,1,0:T(8,128)(2,1)}), bf16[32,16,1280]{2,1,0:T(8,128)(2,1)S(1)}, u32[]{:S(2)}, u32[]{:S(2)}) async-start(bf16[32,16,1280]{2,1,0:T(8,128)(2,1)} %bitcast.9), calls=%async_computation.2 | async-start | bytes 2621440 | tf_op jit(solution)/shard_map/all_to_all | solution.py:353
  112.7 0.5 broadcast.9
  113.2 0.7 reduce.7
  113.9 0.7 reshape.33
  114.5 30.1 %all-to-all-done.2 = bf16[32,16,1280]{2,1,0:T(8,128)(2,1)S(1)} async-done(((bf16[32,16,1280]{2,1,0:T(8,128)(2,1)}), bf16[32,16,1280]{2,1,0:T(8,128)(2,1)S(1)}, u32[]{:S(2)}, u32[]{:S(2)}) %all-to-all-start.2) | async-done | bytes 1310752 | tf_op jit(solution)/shard_map/all_to_all | solution.py:353
  144.7 1.1 copy.14
Async XLA Ops:
  0.6 17.4 %copy-start.1 = (bf16[5,1280]{1,0:T(8,128)(2,1)S(1)}, bf16[5,1280]{1,0:T(8,128)(2,1)}, u32[]{:S(2)}) copy-start(bf16[5,1280]{1,0:T(8,128)(2,1)} %param.17) | copy-start | bytes 38404
  15.0 35.0 %all-to-all-start = ((bf16[32,16,1280]{2,1,0:T(8,128)(2,1)}), bf16[32,16,1280]{2,1,0:T(8,128)(2,1)S(1)}, u32[]{:S(2)}, u32[]{:S(2)}) async-start(bf16[32,16,1280]{2,1,0:T(8,128)(2,1)} %bitcast.7), calls=%async_computation | async-start | bytes 2621440 | tf_op jit(solution)/shard_map/all_to_all | solution.py:353
  50.0 1.1 copy-start
  109.6 35.0 %all-to-all-start.2 = ((bf16[32,16,1280]{2,1,0:T(8,128)(2,1)}), bf16[32,16,1280]{2,1,0:T(8,128)(2,1)S(1)}, u32[]{:S(2)}, u32[]{:S(2)}) async-start(bf16[32,16,1280]{2,1,0:T(8,128)(2,1)} %bitcast.9), calls=%async_computation.2 | async-start | bytes 2621440 | tf_op jit(solution)/shard_map/all_to_all | solution.py:353

commit v2 on v1

--- a/solution.py
+++ b/solution.py
@@ -8,11 +8,13 @@
 from jax.experimental.pallas import tpu as pltpu
 from jax.sharding import PartitionSpec as P
 
+
 COARSE_HOP = 4
 FINE_HOP = 2
 LANES = 128
-CHUNKS = 1
-BLOCK = 128
+PIECES = 3
+CHUNKS = 2
+BLOCK = 256
 
 
 eps = 1e-05
@@ -181,8 +183,8 @@
 
 
 def chain_kernel(
-    near, far, classes, block,
-    x_ref, onehot_ref, ws_in, wt_in, we_in, ws_out, wt_out, we_out, dec_ref,
+    near, far, classes, block, chunk,
+    x_ref, target_ref, before_ref, ws_in, wt_in, we_in, ws_out, wt_out, we_out, dec_ref,
     grad_ref, loss_ref,
     mid_a, mid_b, outer_in, carried,
     n_in_a, s_in_a, f_in_a, n_mid_a, s_mid_a, f_mid_a, n_con_a, s_con_a, f_con_a,
@@ -196,24 +198,32 @@
             body(pl.multiple_of(step * block, block))
             return carry
 
-        lax.fori_loop(0, steps, run, 0)
+        if steps == 1:
+            body(0)
+        else:
+            lax.fori_loop(0, steps, run, 0)
 
     def wrap(ref):
         ref[pl.ds(0, near), :] = ref[pl.ds(total, near), :]
         ref[pl.ds(total + near, near), :] = ref[pl.ds(near, near), :]
 
+    def aligned(start, step):
+        return start if isinstance(start, int) else pl.multiple_of(start, step)
+
     def near_rows(ref, start, shift):
-        return ref[pl.ds(pl.multiple_of(start + near + shift, near), block), :]
+        return ref[pl.ds(aligned(start + near + shift, near), block), :]
 
     def far_rows(ref, start, shift):
-        return ref[pl.ds(pl.multiple_of(lax.rem(start + shift, total), block), block), :]
+        if steps == 1:
+            return jnp.concatenate([ref[shift:total, :], ref[:shift, :]])
+        return ref[pl.ds(aligned(lax.rem(start + shift, total), block), block), :]
 
     def enter(start):
         rows = pl.ds(start, block)
         entry = activate(x_ref[rows, :].astype(F32), n_in_a, s_in_a, f_in_a, rows)
         squeezed = product(entry, ws_in[...])
         middle = activate(squeezed, n_mid_a, s_mid_a, f_mid_a, rows)
-        mid_a[pl.ds(pl.multiple_of(start + near, near), block), :] = middle
+        mid_a[pl.ds(aligned(start + near, near), block), :] = middle
 
     each(enter)
     wrap(mid_a)
@@ -248,12 +258,15 @@
         lane = lax.broadcasted_iota(jnp.int32, logits.shape, 1)
         exponent = jnp.where(lane < classes, jnp.exp(logits), 0.0)
         totals = jnp.sum(exponent, axis=-1, keepdims=True)
-        onehot = onehot_ref[rows, :].astype(F32)
+        target = target_ref[rows, :].astype(F32)[:, chunk : chunk + 1]
+        onehot = jnp.where(lane.astype(F32) == target, 1.0, 0.0)
         loss = jnp.log(totals) - jnp.sum(logits * onehot, axis=-1, keepdims=True)
-        loss = jnp.broadcast_to(loss, (block, LANES))
-        for part in range(block // LANES):
-            flat = jnp.transpose(loss[part * LANES : (part + 1) * LANES, :])
-            loss_ref[pl.ds(start // LANES + part, 1), :] = flat[:1, :]
+        pieces = before_ref[rows, :].astype(F32)
+        for part in range(PIECES):
+            piece = loss.astype(BF).astype(F32)
+            pieces = jnp.where(lane == chunk * PIECES + part, piece, pieces)
+            loss = loss - piece
+        loss_ref[rows, :] = pieces.astype(BF)
         dlogits = (32.0 * (exponent / totals - onehot)).astype(BF)
         upward = norm_back(normal, factor, product(dlogits, dec_ref[...]))
         carried[rows, :] = upward
@@ -274,7 +287,7 @@
         upward = carried[rows, :] + back(dentry, n_in_b, s_in_b, f_in_b, rows)
         carried[rows, :] = upward
         dclosing = product_t(upward.astype(BF), we_in[...])
-        mid_b[pl.ds(pl.multiple_of(start + near, near), block), :] = back(
+        mid_b[pl.ds(aligned(start + near, near), block), :] = back(
             dclosing, n_con_a, s_con_a, f_con_a, rows
         ).astype(BF)
 
@@ -296,8 +309,9 @@
     each(inner_back)
 
 
-def run_chains(rows, onehot, weights, near, far, classes, block):
-    count, width = rows.shape
+def run_chains(rows, targets, before, weights, near, far, classes, block, chunk):
+    count = rows.shape[0]
+    width = weights[0].shape[0]
     bottleneck = weights[0].shape[1]
     padded = count + 2 * near
 
@@ -310,12 +324,12 @@
 
     one_block = kept(width) + kept(bottleneck) + kept(bottleneck)
     return pl.pallas_call(
-        functools.partial(chain_kernel, near, far, classes, block),
+        functools.partial(chain_kernel, near, far, classes, block, chunk),
         out_shape=(
             jax.ShapeDtypeStruct((count, width), BF),
-            jax.ShapeDtypeStruct((count // LANES, LANES), F32),
+            jax.ShapeDtypeStruct((count, LANES), BF),
         ),
-        in_specs=[pl.BlockSpec(memory_space=pltpu.VMEM)] * (2 + len(weights)),
+        in_specs=[pl.BlockSpec(memory_space=pltpu.VMEM)] * (3 + len(weights)),
         out_specs=(
             pl.BlockSpec(memory_space=pltpu.VMEM),
             pl.BlockSpec(memory_space=pltpu.VMEM),
@@ -332,7 +346,7 @@
         cost_estimate=pl.CostEstimate(
             flops=count * 36 * width * bottleneck, bytes_accessed=24 << 20, transcendentals=0
         ),
-    )(rows, onehot, *weights)
+    )(rows, targets, before, *weights)
 
 
 def on_device_chains(chunks, block, activations, targets, *weights):
@@ -353,16 +367,34 @@
         moved = lax.all_to_all(shaped, axes, 0, 0, tiled=True)
         return moved.reshape(values.shape)
 
-    grads, losses = [], []
-    lane = jnp.arange(LANES, dtype=jnp.int32)
+    spare = jnp.zeros((part, LANES - chunks), BF)
+    target_tile = jnp.concatenate([targets.reshape(chunks, part).T.astype(BF), spare], axis=1)
+    there = []
     for chunk in range(chunks):
-        piece = slice(chunk * part, (chunk + 1) * part)
-        there = spread(activations[piece])
-        onehot = (spread(targets[piece])[:, None] == lane[None, :]).astype(BF)
-        grad, loss = run_chains(there, onehot, weights, near, far, classes, block)
-        grads.append(spread(grad))
-        losses.append(spread(loss.reshape(part)))
-    return (jnp.concatenate(grads), jnp.concatenate(losses))
+        piece = activations[chunk * part : (chunk + 1) * part]
+        if chunk == 0:
+            piece = jnp.concatenate([piece, target_tile], axis=1)
+        there.append(spread(piece))
+    target_tile = there[0][:, width:]
+    losses = jnp.zeros((part, LANES), BF)
+    result = None
+    for chunk in range(chunks):
+        piece = there[chunk][:, :width]
+        grad, losses = run_chains(
+            piece, target_tile, losses, weights, near, far, classes, block, chunk
+        )
+        if chunk == chunks - 1:
+            grad = jnp.concatenate([grad, losses], axis=1)
+        home = spread(grad)
+        if chunk == chunks - 1:
+            losses = home[:, width:].astype(F32)
+        place = ((chunk * part, rows - (chunk + 1) * part, 0), (0, 0, 0))
+        if result is None:
+            result = lax.pad(home[:, :width], jnp.zeros((), BF), place)
+        else:
+            result = lax.dynamic_update_slice(result, home[:, :width], (chunk * part, 0))
+    summed = losses[:, : chunks * PIECES].reshape(part, chunks, PIECES).sum(axis=2)
+    return (result, summed.T.reshape(rows))
 
 
 def chains_fit(mesh, rows, chunks, block):
@@ -372,7 +404,7 @@
         return False
     each = part // devices
     far = COARSE_HOP * mesh.shape["fine"] * each
-    return (FINE_HOP * each) % 16 == 0 and block % (FINE_HOP * each) == 0 and far % block == 0
+    return (FINE_HOP * each) % 16 == 0 and block % (FINE_HOP * each) == 0 and chunks * PIECES <= LANES and (far % block == 0 or part == block)
 
 
 def solution(mesh):
@@ -391,11 +423,12 @@
 
     def step(activations, *others):
         rows = activations.shape[0] // mesh.size
-        body = on_device
-        if chains_fit(mesh, rows, CHUNKS, BLOCK):
-            body = functools.partial(on_device_chains, CHUNKS, BLOCK)
-        return jax.shard_map(
+        chained = chains_fit(mesh, rows, CHUNKS, BLOCK)
+        body = functools.partial(on_device_chains, CHUNKS, BLOCK) if chained else on_device
+
+        spread = jax.shard_map(
             body, mesh=mesh, in_specs=in_specs, out_specs=out_specs, check_vma=False
-        )(activations, *others)
+        )
+        return spread(activations, *others)
 
     return step

time: 146 us -> 126 us (0.86)
  waiting for transfers between devices: 59.3 us -> 17.2 us
  blocking collectives: 23.2 us -> 51.4 us
  Pallas kernels: 48.2 us -> 40.1 us
    all_to_all x2, waiting for transfers between devices: 59.3 us -> 17.2 us  [spread(): moved = lax.all_to_all(shaped, axes, 0, 0, tiled=True)]
    all_to_all x2, blocking collectives: 23.2 us -> 51.4 us  [spread(): moved = lax.all_to_all(shaped, axes, 0, 0, tiled=True)]
    pallas_call x1 -> x2, Pallas kernels: 48.2 us -> 40.1 us  [run_chains(): pl.pallas_call(functools.partial(chain_kernel, near, far, classes, block,...]
    slice x0 -> x5, local copies, waits for them, and re-layouts: none -> 3.77 us  [the longest x1 2.2 us: on_device_chains(): piece = activations[chunk * part:(chunk + 1) * part]]
    all_to_all x4 -> x0, local copies, waits for them, and re-layouts: 2.54 us -> none  [spread(): moved = lax.all_to_all(shaped, axes, 0, 0, tiled=True)]
  transfers between devices with their start and end apart: 2 -> 2, of which waited for: 2 -> 1; matrix products, arithmetic and copies ran while one was open for 3% -> 3% of each run, Pallas kernels for 0% -> 16%
where the time goes in v2:
time: 126 us
  blocking collectives  51.4 us (41%)
  Pallas kernels  40.1 us (32%)
  waiting for transfers between devices  17.2 us (14%)
  local copies, waits for them, and re-layouts  7.16 us (6%)
  starting transfers between devices  6.3 us (5%)
  other arithmetic  3.04 us (2%)
    all_to_all x2, blocking collectives, spread(): moved = lax.all_to_all(shaped, axes, 0, 0, tiled=True)  51.4 us
    pallas_call x2, Pallas kernels, run_chains(): pl.pallas_call(functools.partial(chain_kernel, near, far, classes, block,...  40.1 us
    all_to_all x2, waiting for transfers between devices, spread(): moved = lax.all_to_all(shaped, axes, 0, 0, tiled=True)  17.2 us
    all_to_all x2, starting transfers between devices, spread(): moved = lax.all_to_all(shaped, axes, 0, 0, tiled=True)  6.3 us
  transfers between devices with their start and end apart: 2, of which 1 were waited for; matrix products, arithmetic and copies ran while one was open for 3% of the time, Pallas kernels for 16%

profile of v2, /device:TPU:1, one launch (start us, length us, event | category | flops | bytes accessed | tf_op | source)
XLA Modules:
  0.0 125.9 jit_solution(13558448095323941399)
XLA Ops:
  0.6 0.7 convert_element_type.12
  1.3 0.1 copy.17
  1.5 2.2 %fusion = (bf16[256,1280]{1,0:T(8,128)(2,1)S(1)}, bf16[32,8,1280]{2,1,0:T(8,128)(2,1)}) fusion(bf16[512,1280]{1,0:T(8,128)(2,1)} %param.9), kind=kLoop, calls=%fused_computation.3 | loop fusion | bytes 2621440 | tf_op jit(solution)/shard_map/slice | solution.py:374
  3.7 0.3 concatenate.7
  4.0 0.0 copy-start.1
  4.0 26.3 %all_to_all.20 = bf16[32,8,1408]{2,1,0:T(8,128)(2,1)S(1)} all-to-all(bf16[32,8,1408]{2,1,0:T(8,128)(2,1)S(1)} %bitcast.20), channel_id=1, replica_groups=mesh['coarse'=8,'fine'=4] {'coarse','fine'}, dimensions={0} | all-to-all | bytes 1441792 | tf_op jit(solution)/shard_map/all_to_all | solution.py:367
  30.3 3.2 %all-to-all-start.2 = ((bf16[32,8,1280]{2,1,0:T(8,128)(2,1)}), bf16[32,8,1280]{2,1,0:T(8,128)(2,1)S(1)}, u32[]{:S(2)}, u32[]{:S(2)}) async-start(bf16[32,8,1280]{2,1,0:T(8,128)(2,1)} %get-tuple-element.13), calls=%async_computation.2 | async-start | bytes 1310720 | tf_op jit(solution)/shard_map/all_to_all | solution.py:367
  33.5 0.0 copy-done.1
  33.5 0.8 pad.5.dec_ref
  34.2 0.6 slice.28.target_ref
  34.9 0.9 slice.27.x_ref
  35.8 0.6 broadcast_in_dim.7.before_ref
  36.4 20.1 %shard_map.104 = (bf16[256,1280]{1,0:T(8,128)(2,1)}, bf16[256,128]{1,0:T(8,128)(2,1)}) custom-call(bf16[256,1280]{1,0:T(8,128)(2,1)} %slice.27.x_ref, bf16[256,128]{1,0:T(8,128)(2,1)} %slice.28.target_ref, bf16[256,128]{1,0:T(8,128)(2,1)} %broadcast_in_dim.7.before_ref, bf16[1280,640]{1,0:T(8,128)(2,1)} %ws_in.3, bf16[3,640,640]{2,1,0:T(8,128)(2,1)} %wt_in.3, ...), custom_call_target="tpu_custom_call" | custom-call | flops 7549747200 | bytes 25165824 | tf_op jit(solution)/shard_map/pallas_call | solution.py:326
  56.5 0.0 all-to-all-done.2
  56.5 0.0 copy-start
  56.5 0.8 copy-done
  57.4 20.0 %shard_map.105 = (bf16[256,1280]{1,0:T(8,128)(2,1)}, bf16[256,128]{1,0:T(8,128)(2,1)}) custom-call(bf16[256,1280]{1,0:T(8,128)(2,1)} %bitcast.22, bf16[256,128]{1,0:T(8,128)(2,1)} %slice.28.target_ref, bf16[256,128]{1,0:T(8,128)(2,1)} %get-tuple-element.7.before_ref, bf16[1280,640]{1,0:T(8,128)(2,1)} %ws_in.3, bf16[3,640,640]{2,1,0:T(8,128)(2,1)} %wt_in.3, ...), custom_call_target="tpu_custom_call" | custom-call | flops 7549747200 | bytes 25165824 | tf_op jit(solution)/shard_map/pallas_call | solution.py:326
  77.3 1.2 maximum_bitcast_fusion
  78.5 25.1 %all_to_all.21 = bf16[32,8,1408]{2,1,0:T(8,128)(2,1)S(1)} all-to-all(bf16[32,8,1408]{2,1,0:T(8,128)(2,1)S(1)} %maximum_bitcast_fusion), channel_id=1, replica_groups=mesh['coarse'=8,'fine'=4] {'coarse','fine'}, dimensions={0} | all-to-all | bytes 1441792 | tf_op jit(solution)/shard_map/all_to_all | solution.py:367
  103.6 3.2 %all-to-all-start.1 = ((bf16[32,8,1280]{2,1,0:T(8,128)(2,1)}), bf16[32,8,1280]{2,1,0:T(8,128)(2,1)S(1)}, u32[]{:S(2)}, u32[]{:S(2)}) async-start(bf16[32,8,1280]{2,1,0:T(8,128)(2,1)} %bitcast.3), calls=%async_computation.1 | async-start | bytes 1310720 | tf_op jit(solution)/shard_map/all_to_all | solution.py:367
  106.8 0.1 copy.19
  106.9 0.6 copy.20
  107.5 17.2 %all-to-all-done.1 = bf16[32,8,1280]{2,1,0:T(8,128)(2,1)S(1)} async-done(((bf16[32,8,1280]{2,1,0:T(8,128)(2,1)}), bf16[32,8,1280]{2,1,0:T(8,128)(2,1)S(1)}, u32[]{:S(2)}, u32[]{:S(2)}) %all-to-all-start.1) | async-done | bytes 655392 | tf_op jit(solution)/shard_map/all_to_all | solution.py:367
  124.8 1.1 pad_maximum_fusion
  (6 shorter events, 0.1 us)
Async XLA Ops:
  4.0 29.5 %copy-start.1 = (bf16[5,1280]{1,0:T(8,128)(2,1)S(1)}, bf16[5,1280]{1,0:T(8,128)(2,1)}, u32[]{:S(2)}) copy-start(bf16[5,1280]{1,0:T(8,128)(2,1)} %param.17) | copy-start | bytes 38404
  30.3 26.2 %all-to-all-start.2 = ((bf16[32,8,1280]{2,1,0:T(8,128)(2,1)}), bf16[32,8,1280]{2,1,0:T(8,128)(2,1)S(1)}, u32[]{:S(2)}, u32[]{:S(2)}) async-start(bf16[32,8,1280]{2,1,0:T(8,128)(2,1)} %get-tuple-element.13), calls=%async_computation.2 | async-start | bytes 1310720 | tf_op jit(solution)/shard_map/all_to_all | solution.py:367
  56.5 0.8 copy-start
  103.6 21.2 %all-to-all-start.1 = ((bf16[32,8,1280]{2,1,0:T(8,128)(2,1)}), bf16[32,8,1280]{2,1,0:T(8,128)(2,1)S(1)}, u32[]{:S(2)}, u32[]{:S(2)}) async-start(bf16[32,8,1280]{2,1,0:T(8,128)(2,1)} %bitcast.3), calls=%async_computation.1 | async-start | bytes 1310720 | tf_op jit(solution)/shard_map/all_to_all | solution.py:367

commit v3 on v0

--- a/solution.py
+++ b/solution.py
@@ -1,11 +1,22 @@
+import functools
 import math
 
 import jax
 import jax.numpy as jnp
 from jax import lax
+from jax.experimental import pallas as pl
+from jax.experimental.pallas import tpu as pltpu
 from jax.sharding import PartitionSpec as P
 
+
 COARSE_HOP = 4
+FINE_HOP = 2
+LANES = 128
+PIECES = 3
+CHUNKS = 2
+BLOCK = 256
+WHOLE_VMEM = 60 * 1024 * 1024
+SMALL_VMEM = 8 << 20
 
 
 eps = 1e-05
@@ -154,6 +165,318 @@
     return (gradient_result.astype(jnp.bfloat16), token_loss)
 
 
+BF = jnp.bfloat16
+F32 = jnp.float32
+ROOT_HALF = math.sqrt(0.5)
+BELL = math.sqrt(2.0 / math.pi)
+
+
+def scaled_norm(values, scale):
+    average = jnp.mean(values, axis=-1, keepdims=True)
+    centred = values - average
+    factor = lax.rsqrt(jnp.mean(centred * centred, axis=-1, keepdims=True) + eps)
+    return (centred * (factor * scale), factor)
+
+
+def activate(values, kept, rows):
+    scaled_ref, slope_ref, factor_ref = kept
+    scaled, factor = scaled_norm(values, ROOT_HALF)
+    half = ROOT_HALF * lax.erf(scaled) + ROOT_HALF
+    scaled_ref[rows, :] = scaled
+    slope_ref[rows, :] = half + scaled * (BELL * jnp.exp(-(scaled * scaled)))
+    factor_ref[rows, :] = jnp.broadcast_to(factor, (factor.shape[0], LANES))
+    return (scaled * half).astype(BF)
+
+
+def back(upward, kept, rows):
+    scaled_ref, slope_ref, factor_ref = kept
+    scaled = scaled_ref[rows, :]
+    through = slope_ref[rows, :] * upward
+    mean = jnp.mean(through, axis=-1, keepdims=True)
+    along = 2.0 * jnp.mean(through * scaled, axis=-1, keepdims=True)
+    return (through - mean - scaled * along) * (factor_ref[rows, :][:, :1] * ROOT_HALF)
+
+
+def chain_kernel(near, far, block, chunk, last, *refs):
+    refs = list(refs)
+    first_far = refs.pop(0)
+    x_far = refs.pop(0) if chunk else first_far
+    before_ref = refs.pop(0) if chunk else None
+    *weights_far, dec_ref = refs[:7]
+    refs = refs[7:]
+    grad_ref = refs.pop(0)
+    loss_ref = None if last else refs.pop(0)
+    x_ref, ws_in, wt_in, we_in, ws_out, wt_out, we_out, target_ref = refs[:8]
+    dec_pad, mid_a, mid_b, outer_in, carried = refs[8:13]
+    kept = [refs[start : start + 3] for start in range(13, 31, 3)]
+    in_a, mid_kept_a, con_a, in_b, mid_kept_b, con_b = kept
+    sems = refs[31]
+    total, width = x_ref.shape
+    wide, classes = pl.ds(0, width), dec_ref.shape[0]
+    starts = range(0, total, block)
+    sources = [x_far.at[:, wide]] + weights_far + [first_far.at[:, pl.ds(width, LANES)]]
+    copies = [
+        pltpu.make_async_copy(source, target, sems.at[index])
+        for index, (source, target) in enumerate(zip(sources, refs[:8]))
+    ]
+    for copy in copies:
+        copy.start()
+
+    dec_pad[...] = jnp.zeros_like(dec_pad)
+    dec_pad[pl.ds(0, classes), :] = dec_ref[...]
+
+    def wrap(ref):
+        ref[pl.ds(0, near), :] = ref[pl.ds(total, near), :]
+        ref[pl.ds(total + near, near), :] = ref[pl.ds(near, near), :]
+
+    def near_rows(ref, start, shift):
+        return ref[pl.ds(start + near + shift, block), :]
+
+    def far_rows(ref, start, shift):
+        at = (start + shift) % total
+        if at + block <= total:
+            return ref[pl.ds(at, block), :]
+        return jnp.concatenate([ref[at:total, :], ref[: at + block - total, :]])
+
+    def conv(behind, here, ahead, taps):
+        return product(
+            jnp.concatenate([behind, here, ahead], axis=1), taps[...].reshape(-1, taps.shape[2])
+        )
+
+    def conv_back(behind, here, ahead, taps):
+        return product_t(
+            jnp.concatenate([ahead, here, behind], axis=1),
+            jnp.concatenate([taps[0], taps[1], taps[2]], axis=1),
+        )
+
+    copies[0].wait()
+    copies[1].wait()
+    for start in starts:
+        rows = pl.ds(start, block)
+        entry = activate(x_ref[rows, wide].astype(F32), in_a, rows)
+        middle = activate(product(entry, ws_in[...]), mid_kept_a, rows)
+        mid_a[pl.ds(start + near, block), :] = middle
+    wrap(mid_a)
+
+    for copy in copies[2:5]:
+        copy.wait()
+    for start in starts:
+        rows = pl.ds(start, block)
+        shifted = [near_rows(mid_a, start, shift) for shift in (-near, 0, near)]
+        closing = activate(conv(*shifted, wt_in), con_a, rows)
+        following = (x_ref[rows, wide].astype(F32) + product(closing, we_in[...])).astype(BF)
+        outer_in[rows, :] = following
+        entry = activate(following.astype(F32), in_b, rows)
+        mid_b[rows, :] = activate(product(entry, ws_out[...]), mid_kept_b, rows)
+
+    for copy in copies[5:]:
+        copy.wait()
+    for start in starts:
+        rows = pl.ds(start, block)
+        shifted = [far_rows(mid_b, start, shift) for shift in (-far, 0, far)]
+        closing = activate(conv(*shifted, wt_out), con_b, rows)
+        final = (outer_in[rows, :].astype(F32) + product(closing, we_out[...])).astype(BF)
+        normal, factor = scaled_norm(final.astype(F32), 1.0)
+        logits = product_t(normal.astype(BF), dec_pad[...])
+        lane = lax.broadcasted_iota(jnp.int32, logits.shape, 1)
+        exponent = jnp.where(lane < classes, jnp.exp(logits), 0.0)
+        totals = jnp.sum(exponent, axis=-1, keepdims=True)
+        target = target_ref[rows, :].astype(F32)[:, chunk : chunk + 1]
+        onehot = jnp.where(lane.astype(F32) == target, 1.0, 0.0)
+        loss = jnp.log(totals) - jnp.sum(logits * onehot, axis=-1, keepdims=True)
+        pieces = before_ref[rows, :].astype(F32) if chunk else jnp.zeros_like(logits)
+        for part in range(PIECES):
+            piece = loss.astype(BF).astype(F32)
+            pieces = jnp.where(lane == chunk * PIECES + part, piece, pieces)
+            loss = loss - piece
+        if last:
+            grad_ref[rows, pl.ds(width, LANES)] = pieces.astype(BF)
+        else:
+            loss_ref[rows, :] = pieces.astype(BF)
+        dlogits = (32.0 * (exponent / totals - onehot)).astype(BF)
+        upward = norm_back(normal, factor, product(dlogits, dec_pad[...]))
+        carried[rows, :] = upward
+        dclosing = product_t(upward.astype(BF), we_out[...])
+        mid_a[rows, :] = back(dclosing, con_b, rows).astype(BF)
+
+    for start in starts:
+        rows = pl.ds(start, block)
+        shifted = [far_rows(mid_a, start, shift) for shift in (-far, 0, far)]
+        dmiddle = conv_back(*shifted, wt_out)
+        dsqueezed = back(dmiddle, mid_kept_b, rows).astype(BF)
+        upward = carried[rows, :] + back(product_t(dsqueezed, ws_out[...]), in_b, rows)
+        carried[rows, :] = upward
+        dclosing = product_t(upward.astype(BF), we_in[...])
+        mid_b[pl.ds(start + near, block), :] = back(dclosing, con_a, rows).astype(BF)
+    wrap(mid_b)
+
+    for start in starts:
+        rows = pl.ds(start, block)
+        shifted = [near_rows(mid_b, start, shift) for shift in (-near, 0, near)]
+        dmiddle = conv_back(*shifted, wt_in)
+        dsqueezed = back(dmiddle, mid_kept_a, rows).astype(BF)
+        upward = carried[rows, :] + back(product_t(dsqueezed, ws_in[...]), in_a, rows)
+        grad_ref[rows, wide] = upward.astype(BF)
+
+
+VMEM = pl.BlockSpec(memory_space=pltpu.VMEM)
+ANY = pl.BlockSpec(memory_space=pl.ANY)
+
+
+def run_chains(first, rows, before, weights, near, far, block, chunk, last):
+    count = first.shape[0]
+    width, bottleneck = weights[0].shape
+    padded = count + 2 * near
+    tile = jax.ShapeDtypeStruct((count, LANES), BF)
+    if last:
+        out_shape = (jax.ShapeDtypeStruct((count, width + LANES), BF),)
+    else:
+        out_shape = (jax.ShapeDtypeStruct((count, width), BF), tile)
+
+    def kept(size):
+        return [
+            pltpu.VMEM((count, size), F32),
+            pltpu.VMEM((count, size), F32),
+            pltpu.VMEM((count, LANES), F32),
+        ]
+
+    one_block = kept(width) + kept(bottleneck) + kept(bottleneck)
+    operands = ((first, rows, before) if chunk else (first,)) + weights
+    return pl.pallas_call(
+        functools.partial(chain_kernel, near, far, block, chunk, last),
+        out_shape=out_shape,
+        in_specs=[ANY] * (2 if chunk else 1) + [VMEM] * (1 if chunk else 0) + [ANY] * 6 + [VMEM],
+        out_specs=(VMEM,) * len(out_shape),
+        scratch_shapes=[pltpu.VMEM((count, width), BF)]
+        + [pltpu.VMEM(weight.shape, BF) for weight in weights[:6]]
+        + [
+            pltpu.VMEM((count, LANES), BF),
+            pltpu.VMEM((LANES, width), BF),
+            pltpu.VMEM((padded, bottleneck), BF),
+            pltpu.VMEM((padded, bottleneck), BF),
+            pltpu.VMEM((count, width), BF),
+            pltpu.VMEM((count, width), F32),
+        ]
+        + one_block
+        + one_block
+        + [pltpu.SemaphoreType.DMA((8,))],
+        compiler_params=pltpu.CompilerParams(vmem_limit_bytes=WHOLE_VMEM),
+        cost_estimate=pl.CostEstimate(
+            flops=count * 36 * width * bottleneck, bytes_accessed=24 << 20, transcendentals=0
+        ),
+    )(*operands)
+
+
+def pack_kernel(x_ref, target_ref, *refs):
+    outs, sems = refs[:-1], refs[-1]
+    part, width = outs[-1].shape
+    copies = []
+    for chunk, out in enumerate(outs):
+        source = x_ref.at[pl.ds(chunk * part, part), :]
+        copies.append(pltpu.make_async_copy(source, out.at[:, pl.ds(0, width)], sems.at[chunk]))
+        copies[-1].start()
+    lane = lax.broadcasted_iota(jnp.int32, (LANES, LANES), 1)
+    for start in range(0, part, LANES):
+        tile = jnp.zeros((LANES, LANES), F32)
+        for chunk in range(len(outs)):
+            row = target_ref[pl.ds((chunk * part + start) // LANES, 1), :].astype(F32)
+            column = jnp.transpose(jnp.broadcast_to(row, (LANES, LANES)))
+            tile = jnp.where(lane == chunk, column, tile)
+        outs[0][pl.ds(start, LANES), pl.ds(width, LANES)] = tile.astype(BF)
+    for copy in copies:
+        copy.wait()
+
+
+def pack(activations, targets, chunks):
+    rows, width = activations.shape
+    part = rows // chunks
+    widths = [width + LANES] + [width] * (chunks - 1)
+    return pl.pallas_call(
+        pack_kernel,
+        out_shape=tuple(jax.ShapeDtypeStruct((part, size), BF) for size in widths),
+        in_specs=[ANY, VMEM],
+        out_specs=(VMEM,) * chunks,
+        scratch_shapes=[pltpu.SemaphoreType.DMA((chunks,))],
+        compiler_params=pltpu.CompilerParams(vmem_limit_bytes=WHOLE_VMEM),
+    )(activations, targets.reshape(rows // LANES, LANES))
+
+
+def unpack_kernel(*refs):
+    *pieces, out_ref, loss_ref, sems = refs
+    part, width = pieces[-1].shape[0], out_ref.shape[1]
+    copies = []
+    for chunk, piece in enumerate(pieces):
+        place = out_ref.at[pl.ds(chunk * part, part), :]
+        copies.append(pltpu.make_async_copy(piece.at[:, pl.ds(0, width)], place, sems.at[chunk]))
+        copies[-1].start()
+    for start in range(0, part, LANES):
+        tile = pieces[-1][pl.ds(start, LANES), pl.ds(width, LANES)].astype(F32)
+        flat = jnp.transpose(tile)
+        for chunk in range(len(pieces)):
+            lines = [flat[chunk * PIECES + part : chunk * PIECES + part + 1] for part in range(PIECES)]
+            loss_ref[pl.ds((chunk * pieces[-1].shape[0] + start) // LANES, 1), :] = sum(
+                lines[1:], lines[0]
+            )
+    for copy in copies:
+        copy.wait()
+
+
+def unpack(homes, width):
+    chunks, part = len(homes), homes[0].shape[0]
+    rows = chunks * part
+    result, losses = pl.pallas_call(
+        unpack_kernel,
+        out_shape=(
+            jax.ShapeDtypeStruct((rows, width), BF),
+            jax.ShapeDtypeStruct((rows // LANES, LANES), F32),
+        ),
+        in_specs=[VMEM] * chunks,
+        out_specs=(ANY, VMEM),
+        scratch_shapes=[pltpu.SemaphoreType.DMA((chunks,))],
+        compiler_params=pltpu.CompilerParams(vmem_limit_bytes=SMALL_VMEM),
+    )(*homes)
+    return (result, losses.reshape(rows))
+
+
+def on_device_chains(chunks, block, activations, targets, *weights):
+    axes = ("coarse", "fine")
+    devices = lax.axis_size(axes)
+    rows, width = activations.shape
+    part = rows // chunks
+    each = part // devices
+    near = FINE_HOP * each
+    far = COARSE_HOP * lax.axis_size("fine") * each
+
+    def spread(values):
+        shaped = values.reshape((devices, each) + values.shape[1:])
+        moved = lax.all_to_all(shaped, axes, 0, 0, tiled=True)
+        return moved.reshape(values.shape)
+
+    there = []
+    for piece in pack(activations, targets, chunks):
+        there.append(spread(piece))
+    losses = None
+    homes = []
+    for chunk in range(chunks):
+        grad, *losses = run_chains(
+            there[0], there[chunk], *(losses or [None]), weights, near, far, block, chunk,
+            chunk == chunks - 1,
+        )
+        homes.append(spread(grad))
+    return unpack(homes, width)
+
+
+def chains_fit(mesh, rows, chunks, block):
+    devices = mesh.shape["coarse"] * mesh.shape["fine"]
+    part = rows // chunks
+    if rows % chunks or part % devices or part % block or part % LANES:
+        return False
+    each = part // devices
+    far = COARSE_HOP * mesh.shape["fine"] * each
+    near = FINE_HOP * each
+    return near % 16 == 0 and far % 16 == 0 and chunks * PIECES <= LANES
+
+
 def solution(mesh):
     in_specs = (
         P(("coarse", "fine"), None),
@@ -167,6 +490,15 @@
         P(),
     )
     out_specs = (P(("coarse", "fine"), None), P(("coarse", "fine")))
-    return jax.shard_map(
-        on_device, mesh=mesh, in_specs=in_specs, out_specs=out_specs, check_vma=False
-    )
+
+    def step(activations, *others):
+        rows = activations.shape[0] // mesh.size
+        chained = chains_fit(mesh, rows, CHUNKS, BLOCK)
+        body = functools.partial(on_device_chains, CHUNKS, BLOCK) if chained else on_device
+
+        spread = jax.shard_map(
+            body, mesh=mesh, in_specs=in_specs, out_specs=out_specs, check_vma=False
+        )
+        return spread(activations, *others)
+
+    return step

time: 169 us -> 103 us (0.61)
  waiting for transfers between devices: 111 us -> 0.08 us
  blocking collectives: 0 us -> 51.9 us
  Pallas kernels: 0 us -> 40.8 us
  matrix products: 33.1 us -> 0 us
  other arithmetic: 10.2 us -> 0 us
  starting transfers between devices: 13.2 us -> 8.93 us
    ppermute x8 -> x0, waiting for transfers between devices: 111 us -> none  [from_behind(): return lax.ppermute(value, axis, pairs)]
    all_to_all x0 -> x2, blocking collectives: none -> 51.9 us  [spread(): moved = lax.all_to_all(shaped, axes, 0, 0, tiled=True)]
    pallas_call x0 -> x4, Pallas kernels: none -> 40.8 us  [the longest x2 36 us: run_chains(): pl.pallas_call(functools.partial(chain_kernel, near, far, block, chunk, l...]
    dot_general x22 -> x0, matrix products: 33.1 us -> none  [the longest x11 17.5 us: product(): return jnp.dot(leading, trailing, preferred_element_type=jnp.float32)]
    ppermute x8 -> x0, starting transfers between devices: 13.2 us -> none  [from_behind(): return lax.ppermute(value, axis, pairs)]
    all_to_all x0 -> x2, starting transfers between devices: none -> 8.93 us  [spread(): moved = lax.all_to_all(shaped, axes, 0, 0, tiled=True)]
    reduce_sum x8 -> x0, other arithmetic: 4.34 us -> none  [the longest x7 2.63 us: norm_rows(): jnp.mean(centred * centred, axis=-1, keepdims=True) + eps]
    convert_element_type x5 -> x0, other arithmetic: 3.46 us -> none  [the longest x1 1.91 us: on_device(): return (gradient_result.astype(jnp.bfloat16), token_loss)]
  transfers between devices with their start and end apart: 8 -> 2, of which waited for: 6 -> 1; matrix products, arithmetic and copies ran while one was open for 5% -> 0% of each run, Pallas kernels for 0% -> 35%
where the time goes in v3:
time: 103 us; the launch traced here: 102 us
  blocking collectives  51.9 us (50%)
  Pallas kernels  40.8 us (40%)
  starting transfers between devices  8.93 us (9%)
    all_to_all x2, blocking collectives, spread(): moved = lax.all_to_all(shaped, axes, 0, 0, tiled=True)  51.9 us
    pallas_call x2, Pallas kernels, run_chains(): pl.pallas_call(functools.partial(chain_kernel, near, far, block, chunk, l...  36 us
    all_to_all x2, starting transfers between devices, spread(): moved = lax.all_to_all(shaped, axes, 0, 0, tiled=True)  8.93 us
    pallas_call x1, Pallas kernels, pack(): pl.pallas_call(pack_kernel, out_shape=tuple((jax.ShapeDtypeStruct((part,...  3.06 us
  transfers between devices with their start and end apart: 2, of which 1 were waited for; matrix products, arithmetic and copies ran while one was open for 0% of the time, Pallas kernels for 35%

profile of v3, /device:TPU:1, one launch (start us, length us, event | category | flops | bytes accessed | tf_op | source)
XLA Modules:
  0.0 102.5 jit_solution(273293979373978108)
XLA Ops:
  0.6 3.1 %shard_map.104 = (bf16[256,1408]{1,0:T(8,128)(2,1)}, bf16[256,1280]{1,0:T(8,128)(2,1)}) custom-call(bf16[512,1280]{1,0:T(8,128)(2,1)} %x_ref.1, s32[4,128]{1,0:T(4,128)} %bitcast.19), custom_call_target="tpu_custom_call" | custom-call | tf_op jit(solution)/shard_map/pallas_call | solution.py:394
  3.7 26.6 %all_to_all.20 = bf16[32,8,1408]{2,1,0:T(8,128)(2,1)} all-to-all(bf16[32,8,1408]{2,1,0:T(8,128)(2,1)} %bitcast.15), channel_id=1, replica_groups=mesh['coarse'=8,'fine'=4] {'coarse','fine'}, dimensions={0} | all-to-all | bytes 1441792 | tf_op jit(solution)/shard_map/all_to_all | solution.py:452
  30.3 3.2 %all-to-all-start.2 = ((bf16[32,8,1280]{2,1,0:T(8,128)(2,1)}), bf16[32,8,1280]{2,1,0:T(8,128)(2,1)S(1)}, u32[]{:S(2)}, u32[]{:S(2)}) async-start(bf16[32,8,1280]{2,1,0:T(8,128)(2,1)} %bitcast.18), calls=%async_computation.2 | async-start | bytes 1310720 | tf_op jit(solution)/shard_map/all_to_all | solution.py:452
  33.5 17.9 %shard_map.105 = (bf16[256,1280]{1,0:T(8,128)(2,1)}, bf16[256,128]{1,0:T(8,128)(2,1)}) custom-call(bf16[256,1408]{1,0:T(8,128)(2,1)} %bitcast.12, bf16[1280,640]{1,0:T(8,128)(2,1)} %refs_3_.3, bf16[3,640,640]{2,1,0:T(8,128)(2,1)} %refs_4_.3, bf16[640,1280]{1,0:T(8,128)(2,1)} %refs_5_.3, bf16[1280,640]{1,0:T(8,128)(2,1)} %refs_6_.3, ...), custom_call_target="tpu_custom_call" | custom-call | flops 7549747200 | bytes 25165824 | tf_op jit(solution)/shard_map/pallas_call | solution.py:345
  51.4 0.1 all-to-all-done.2
  51.5 0.0 copy-start
  51.5 5.8 %all-to-all-start.1 = ((bf16[32,8,1280]{2,1,0:T(8,128)(2,1)}), bf16[32,8,1280]{2,1,0:T(8,128)(2,1)S(1)}, u32[]{:S(2)}, u32[]{:S(2)}) async-start(bf16[32,8,1280]{2,1,0:T(8,128)(2,1)} %bitcast.17), calls=%async_computation.1 | async-start | bytes 1310720 | tf_op jit(solution)/shard_map/all_to_all | solution.py:452
  57.3 0.0 copy-done
  57.3 18.1 %shard_map.106 = bf16[256,1408]{1,0:T(8,128)(2,1)} custom-call(bf16[256,1408]{1,0:T(8,128)(2,1)} %bitcast.13, bf16[256,1280]{1,0:T(8,128)(2,1)} %bitcast.16, bf16[256,128]{1,0:T(8,128)(2,1)} %get-tuple-element.11.refs_2_, bf16[1280,640]{1,0:T(8,128)(2,1)} %refs_3_.3, bf16[3,640,640]{2,1,0:T(8,128)(2,1)} %refs_4_.3, bf16[640,1280]{1,0:T(8,128)(2,1)} %refs_5_.3, ...), custom_call_target="tpu_custom_call" | custom-call | flops 7549747200 | bytes 25165824 | tf_op jit(solution)/shard_map/pallas_call | solution.py:345
  75.4 0.0 all-to-all-done.1
  75.4 25.3 %all_to_all.21 = bf16[32,8,1408]{2,1,0:T(8,128)(2,1)S(1)} all-to-all(bf16[32,8,1408]{2,1,0:T(8,128)(2,1)} %bitcast.14), channel_id=1, replica_groups=mesh['coarse'=8,'fine'=4] {'coarse','fine'}, dimensions={0} | all-to-all | bytes 1441792 | tf_op jit(solution)/shard_map/all_to_all | solution.py:452
  100.7 1.6 %shard_map.107 = (bf16[512,1280]{1,0:T(8,128)(2,1)}, f32[4,128]{1,0:T(4,128)}) custom-call(bf16[256,1280]{1,0:T(8,128)(2,1)S(1)} %bitcast.11, bf16[256,1408]{1,0:T(8,128)(2,1)S(1)} %bitcast.10), custom_call_target="tpu_custom_call" | custom-call | tf_op jit(solution)/shard_map/pallas_call | solution.py:427
Async XLA Ops:
  30.3 21.2 %all-to-all-start.2 = ((bf16[32,8,1280]{2,1,0:T(8,128)(2,1)}), bf16[32,8,1280]{2,1,0:T(8,128)(2,1)S(1)}, u32[]{:S(2)}, u32[]{:S(2)}) async-start(bf16[32,8,1280]{2,1,0:T(8,128)(2,1)} %bitcast.18), calls=%async_computation.2 | async-start | bytes 1310720 | tf_op jit(solution)/shard_map/all_to_all | solution.py:452
  51.5 5.8 %copy-start = (bf16[32,8,1280]{2,1,0:T(8,128)(2,1)}, bf16[32,8,1280]{2,1,0:T(8,128)(2,1)S(1)}, u32[]{:S(2)}) copy-start(bf16[32,8,1280]{2,1,0:T(8,128)(2,1)S(1)} %all-to-all-done.2) | copy-start | bytes 1966084
  51.5 23.9 %all-to-all-start.1 = ((bf16[32,8,1280]{2,1,0:T(8,128)(2,1)}), bf16[32,8,1280]{2,1,0:T(8,128)(2,1)S(1)}, u32[]{:S(2)}, u32[]{:S(2)}) async-start(bf16[32,8,1280]{2,1,0:T(8,128)(2,1)} %bitcast.17), calls=%async_computation.1 | async-start | bytes 1310720 | tf_op jit(solution)/shard_map/all_to_all | solution.py:452

commit v4 on v3

--- a/solution.py
+++ b/solution.py
@@ -199,27 +199,27 @@
 
 def chain_kernel(near, far, block, chunk, last, *refs):
     refs = list(refs)
-    first_far = refs.pop(0)
-    x_far = refs.pop(0) if chunk else first_far
+    x_far = refs.pop(0)
+    target_ref = refs.pop(0)
     before_ref = refs.pop(0) if chunk else None
     *weights_far, dec_ref = refs[:7]
     refs = refs[7:]
     grad_ref = refs.pop(0)
     loss_ref = None if last else refs.pop(0)
-    x_ref, ws_in, wt_in, we_in, ws_out, wt_out, we_out, target_ref = refs[:8]
-    dec_pad, mid_a, mid_b, outer_in, carried = refs[8:13]
-    kept = [refs[start : start + 3] for start in range(13, 31, 3)]
+    x_ref, ws_in, wt_in, we_in, ws_out, wt_out, we_out = refs[:7]
+    dec_pad, mid_a, mid_b, outer_in, carried = refs[7:12]
+    kept = [refs[start : start + 3] for start in range(12, 30, 3)]
     in_a, mid_kept_a, con_a, in_b, mid_kept_b, con_b = kept
-    sems = refs[31]
+    sems = refs[30]
     total, width = x_ref.shape
     wide, classes = pl.ds(0, width), dec_ref.shape[0]
     starts = range(0, total, block)
-    sources = [x_far.at[:, wide]] + weights_far + [first_far.at[:, pl.ds(width, LANES)]]
+    sources = [x_far] + weights_far
     copies = [
         pltpu.make_async_copy(source, target, sems.at[index])
-        for index, (source, target) in enumerate(zip(sources, refs[:8]))
+        for index, (source, target) in enumerate(zip(sources, refs[:7]))
     ]
-    for copy in copies:
+    for copy in copies[:2]:
         copy.start()
 
     dec_pad[...] = jnp.zeros_like(dec_pad)
@@ -249,11 +249,13 @@
             jnp.concatenate([taps[0], taps[1], taps[2]], axis=1),
         )
 
-    copies[0].wait()
-    copies[1].wait()
+    for copy in copies[:2]:
+        copy.wait()
+    for copy in copies[2:]:
+        copy.start()
     for start in starts:
         rows = pl.ds(start, block)
-        entry = activate(x_ref[rows, wide].astype(F32), in_a, rows)
+        entry = activate(x_ref[rows, :].astype(F32), in_a, rows)
         middle = activate(product(entry, ws_in[...]), mid_kept_a, rows)
         mid_a[pl.ds(start + near, block), :] = middle
     wrap(mid_a)
@@ -264,7 +266,7 @@
         rows = pl.ds(start, block)
         shifted = [near_rows(mid_a, start, shift) for shift in (-near, 0, near)]
         closing = activate(conv(*shifted, wt_in), con_a, rows)
-        following = (x_ref[rows, wide].astype(F32) + product(closing, we_in[...])).astype(BF)
+        following = (x_ref[rows, :].astype(F32) + product(closing, we_in[...])).astype(BF)
         outer_in[rows, :] = following
         entry = activate(following.astype(F32), in_b, rows)
         mid_b[rows, :] = activate(product(entry, ws_out[...]), mid_kept_b, rows)
@@ -323,8 +325,8 @@
 ANY = pl.BlockSpec(memory_space=pl.ANY)
 
 
-def run_chains(first, rows, before, weights, near, far, block, chunk, last):
-    count = first.shape[0]
+def run_chains(rows, carried, weights, near, far, block, chunk, last):
+    count = rows.shape[0]
     width, bottleneck = weights[0].shape
     padded = count + 2 * near
     tile = jax.ShapeDtypeStruct((count, LANES), BF)
@@ -341,16 +343,15 @@
         ]
 
     one_block = kept(width) + kept(bottleneck) + kept(bottleneck)
-    operands = ((first, rows, before) if chunk else (first,)) + weights
+    operands = (rows,) + carried + weights
     return pl.pallas_call(
         functools.partial(chain_kernel, near, far, block, chunk, last),
         out_shape=out_shape,
-        in_specs=[ANY] * (2 if chunk else 1) + [VMEM] * (1 if chunk else 0) + [ANY] * 6 + [VMEM],
+        in_specs=[ANY] + [VMEM] * len(carried) + [ANY] * 6 + [VMEM],
         out_specs=(VMEM,) * len(out_shape),
         scratch_shapes=[pltpu.VMEM((count, width), BF)]
         + [pltpu.VMEM(weight.shape, BF) for weight in weights[:6]]
         + [
-            pltpu.VMEM((count, LANES), BF),
             pltpu.VMEM((LANES, width), BF),
             pltpu.VMEM((padded, bottleneck), BF),
             pltpu.VMEM((padded, bottleneck), BF),
@@ -359,46 +360,12 @@
         ]
         + one_block
         + one_block
-        + [pltpu.SemaphoreType.DMA((8,))],
+        + [pltpu.SemaphoreType.DMA((7,))],
         compiler_params=pltpu.CompilerParams(vmem_limit_bytes=WHOLE_VMEM),
         cost_estimate=pl.CostEstimate(
             flops=count * 36 * width * bottleneck, bytes_accessed=24 << 20, transcendentals=0
         ),
     )(*operands)
-
-
-def pack_kernel(x_ref, target_ref, *refs):
-    outs, sems = refs[:-1], refs[-1]
-    part, width = outs[-1].shape
-    copies = []
-    for chunk, out in enumerate(outs):
-        source = x_ref.at[pl.ds(chunk * part, part), :]
-        copies.append(pltpu.make_async_copy(source, out.at[:, pl.ds(0, width)], sems.at[chunk]))
-        copies[-1].start()
-    lane = lax.broadcasted_iota(jnp.int32, (LANES, LANES), 1)
-    for start in range(0, part, LANES):
-        tile = jnp.zeros((LANES, LANES), F32)
-        for chunk in range(len(outs)):
-            row = target_ref[pl.ds((chunk * part + start) // LANES, 1), :].astype(F32)
-            column = jnp.transpose(jnp.broadcast_to(row, (LANES, LANES)))
-            tile = jnp.where(lane == chunk, column, tile)
-        outs[0][pl.ds(start, LANES), pl.ds(width, LANES)] = tile.astype(BF)
-    for copy in copies:
-        copy.wait()
-
-
-def pack(activations, targets, chunks):
-    rows, width = activations.shape
-    part = rows // chunks
-    widths = [width + LANES] + [width] * (chunks - 1)
-    return pl.pallas_call(
-        pack_kernel,
-        out_shape=tuple(jax.ShapeDtypeStruct((part, size), BF) for size in widths),
-        in_specs=[ANY, VMEM],
-        out_specs=(VMEM,) * chunks,
-        scratch_shapes=[pltpu.SemaphoreType.DMA((chunks,))],
-        compiler_params=pltpu.CompilerParams(vmem_limit_bytes=WHOLE_VMEM),
-    )(activations, targets.reshape(rows // LANES, LANES))
 
 
 def unpack_kernel(*refs):
@@ -452,15 +419,32 @@
         moved = lax.all_to_all(shaped, axes, 0, 0, tiled=True)
         return moved.reshape(values.shape)
 
-    there = []
-    for piece in pack(activations, targets, chunks):
-        there.append(spread(piece))
-    losses = None
+    def gathered(values):
+        parts = values[None]
+        me = lax.axis_index(axes)
+        while parts.shape[0] < devices:
+            distance = parts.shape[0]
+            pairs = [(source, source ^ distance) for source in range(devices)]
+            got = lax.ppermute(parts, axes, pairs)
+            upper = lax.bitwise_and(me, distance) > 0
+            parts = jnp.where(
+                upper, jnp.concatenate([got, parts]), jnp.concatenate([parts, got])
+            )
+        return parts
+
+    there = [spread(activations[:part])]
+    everyone = lax.optimization_barrier(gathered(targets)).reshape(devices, chunks, devices, each)
+    mine = lax.dynamic_slice_in_dim(everyone, lax.axis_index(axes), 1, axis=2)
+    columns = mine.transpose(0, 3, 1, 2).reshape(part, chunks).astype(BF)
+    tile = jnp.pad(columns, ((0, 0), (0, LANES - chunks)))
+    held, tile = lax.optimization_barrier((activations, tile))
+    for chunk in range(1, chunks):
+        there.append(spread(held[chunk * part : (chunk + 1) * part]))
+    losses = ()
     homes = []
     for chunk in range(chunks):
         grad, *losses = run_chains(
-            there[0], there[chunk], *(losses or [None]), weights, near, far, block, chunk,
-            chunk == chunks - 1,
+            there[chunk], (tile, *losses), weights, near, far, block, chunk, chunk == chunks - 1
         )
         homes.append(spread(grad))
     return unpack(homes, width)
@@ -474,7 +458,8 @@
     each = part // devices
     far = COARSE_HOP * mesh.shape["fine"] * each
     near = FINE_HOP * each
-    return near % 16 == 0 and far % 16 == 0 and chunks * PIECES <= LANES
+    paired = devices & (devices - 1) == 0
+    return paired and near % 16 == 0 and far % 16 == 0 and chunks * PIECES <= LANES
 
 
 def solution(mesh):

time: 103 us -> 115 us (1.12)
  blocking collectives: 51.9 us -> 25.3 us
  starting transfers between devices: 8.93 us -> 29.2 us
  waiting for transfers between devices: 0.08 us -> 15.3 us
  local copies, waits for them, and re-layouts: 0.01 us -> 3.92 us
    all_to_all x2 -> x1, blocking collectives: 51.9 us -> 25.3 us  [spread(): moved = lax.all_to_all(shaped, axes, 0, 0, tiled=True)]
    ppermute x0 -> x5, waiting for transfers between devices: none -> 15.3 us  [gathered(): got = lax.ppermute(parts, axes, pairs)]
    all_to_all x2 -> x3, starting transfers between devices: 8.93 us -> 20 us  [spread(): moved = lax.all_to_all(shaped, axes, 0, 0, tiled=True)]
    ppermute x0 -> x5, starting transfers between devices: none -> 9.2 us  [gathered(): got = lax.ppermute(parts, axes, pairs)]
    pallas_call x1 -> x0, Pallas kernels: 3.06 us -> none  [pack(): pl.pallas_call(pack_kernel, out_shape=tuple((jax.ShapeDtypeStruct((part,...]
    reshape x0 -> x2, local copies, waits for them, and re-layouts: none -> 2.98 us  [spread(): shaped = values.reshape((devices, each) + values.shape[1:])]
    pallas_call x2, Pallas kernels: 36 us -> 38.1 us  [run_chains(): pl.pallas_call(functools.partial(chain_kernel, near, far, block, chunk, l...]
  transfers between devices with their start and end apart: 2 -> 8, of which waited for: 1 -> 5; matrix products, arithmetic and copies ran while one was open for 0% -> 2% of each run, Pallas kernels for 35% -> 33%
where the time goes in v4:
time: 115 us; the launch traced here: 114 us
  Pallas kernels  39.7 us (35%)
  starting transfers between devices  29.2 us (25%)
  blocking collectives  25.3 us (22%)
  waiting for transfers between devices  15.3 us (13%)
  local copies, waits for them, and re-layouts  3.92 us (3%)
    pallas_call x2, Pallas kernels, run_chains(): pl.pallas_call(functools.partial(chain_kernel, near, far, block, chunk, l...  38.1 us
    all_to_all x1, blocking collectives, spread(): moved = lax.all_to_all(shaped, axes, 0, 0, tiled=True)  25.3 us
    all_to_all x3, starting transfers between devices, spread(): moved = lax.all_to_all(shaped, axes, 0, 0, tiled=True)  20 us
    ppermute x5, waiting for transfers between devices, gathered(): got = lax.ppermute(parts, axes, pairs)  15.3 us
    ppermute x5, starting transfers between devices, gathered(): got = lax.ppermute(parts, axes, pairs)  9.2 us
    reshape x2, local copies, waits for them, and re-layouts, spread(): shaped = values.reshape((devices, each) + values.shape[1:])  2.98 us
  transfers between devices with their start and end apart: 8, of which 5 were waited for; matrix products, arithmetic and copies ran while one was open for 2% of the time, Pallas kernels for 33%

profile of v4, /device:TPU:1, one launch (start us, length us, event | category | flops | bytes accessed | tf_op | source)
XLA Modules:
  0.0 114.4 jit_solution(12820639604993383543)
XLA Ops:
  0.6 0.0 copy-start
  0.6 0.0 copy-start.3
  0.6 2.1 %slice_bitcast_fusion.1 = bf16[32,8,1280]{2,1,0:T(8,128)(2,1)} fusion(bf16[512,1280]{1,0:T(8,128)(2,1)} %param.9), kind=kLoop, calls=%fused_computation.1 | loop fusion | bytes 1310720 | tf_op jit(solution)/shard_map/reshape | solution.py:418
  2.7 7.1 %all-to-all-start = ((bf16[32,8,1280]{2,1,0:T(8,128)(2,1)}), bf16[32,8,1280]{2,1,0:T(8,128)(2,1)S(1)}, u32[]{:S(2)}, u32[]{:S(2)}) async-start(bf16[32,8,1280]{2,1,0:T(8,128)(2,1)} %slice_bitcast_fusion.1), calls=%async_computation | async-start | bytes 1310720 | tf_op jit(solution)/shard_map/all_to_all | solution.py:419
  9.8 0.0 copy-done.3
  9.8 1.4 %collective-permute-start = (s32[1,512]{1,0:T(1,128)S(1)}, s32[1,512]{1,0:T(1,128)S(1)}, u32[]{:S(2)}, u32[]{:S(2)}) collective-permute-start(s32[1,512]{1,0:T(1,128)S(1)} %bitcast.24), channel_id=1, source_target_pairs={{0,1},{1,0},{2,3},{3,2},{4,5},{5,4},{6,7},{7,6},{8,9},{9,8},{10,11... | collective-permute-start | bytes 6152 | tf_op jit(solution)/shard_map/ppermute | solution.py:428
  11.2 9.4 %collective-permute-done = s32[1,512]{1,0:T(1,128)S(1)} collective-permute-done((s32[1,512]{1,0:T(1,128)S(1)}, s32[1,512]{1,0:T(1,128)S(1)}, u32[]{:S(2)}, u32[]{:S(2)}) %collective-permute-start) | collective-permute-done | bytes 2080 | tf_op jit(solution)/shard_map/ppermute | solution.py:428
  20.7 4.0 %collective-permute-start.1 = (s32[2,512]{1,0:T(2,128)S(1)}, s32[2,512]{1,0:T(2,128)S(1)}, u32[]{:S(2)}, u32[]{:S(2)}) collective-permute-start(s32[2,512]{1,0:T(2,128)S(1)} %add_select_fusion.4), channel_id=1, source_target_pairs={{0,2},{1,3},{2,0},{3,1},{4,6},{5,7},{6,4},{7,5},{8,10},{9,11},{10,... | collective-permute-start | bytes 12296 | tf_op jit(solution)/shard_map/ppermute | solution.py:428
  24.7 2.0 %collective-permute-done.1 = s32[2,512]{1,0:T(2,128)S(1)} collective-permute-done((s32[2,512]{1,0:T(2,128)S(1)}, s32[2,512]{1,0:T(2,128)S(1)}, u32[]{:S(2)}, u32[]{:S(2)}) %collective-permute-start.1) | collective-permute-done | bytes 4128 | tf_op jit(solution)/shard_map/ppermute | solution.py:428
  26.7 1.4 %collective-permute-start.2 = (s32[4,512]{1,0:T(4,128)S(1)}, s32[4,512]{1,0:T(4,128)S(1)}, u32[]{:S(2)}, u32[]{:S(2)}) collective-permute-start(s32[4,512]{1,0:T(4,128)S(1)} %add_select_fusion.3), channel_id=1, source_target_pairs={{0,4},{1,5},{2,6},{3,7},{4,0},{5,1},{6,2},{7,3},{8,12},{9,13},{10,... | collective-permute-start | bytes 24584 | tf_op jit(solution)/shard_map/ppermute | solution.py:428
  28.1 0.8 collective-permute-done.2
  28.9 1.2 %collective-permute-start.3 = (s32[8,512]{1,0:T(8,128)S(1)}, s32[8,512]{1,0:T(8,128)S(1)}, u32[]{:S(2)}, u32[]{:S(2)}) collective-permute-start(s32[8,512]{1,0:T(8,128)S(1)} %add_select_fusion.2), channel_id=1, source_target_pairs={{0,8},{1,9},{2,10},{3,11},{4,12},{5,13},{6,14},{7,15},{8,0},{9,1},... | collective-permute-start | bytes 49160 | tf_op jit(solution)/shard_map/ppermute | solution.py:428
  30.2 1.4 %collective-permute-done.3 = s32[8,512]{1,0:T(8,128)S(1)} collective-permute-done((s32[8,512]{1,0:T(8,128)S(1)}, s32[8,512]{1,0:T(8,128)S(1)}, u32[]{:S(2)}, u32[]{:S(2)}) %collective-permute-start.3) | collective-permute-done | bytes 16416 | tf_op jit(solution)/shard_map/ppermute | solution.py:428
  31.6 1.2 %collective-permute-start.4 = (s32[16,512]{1,0:T(8,128)S(1)}, s32[16,512]{1,0:T(8,128)S(1)}, u32[]{:S(2)}, u32[]{:S(2)}) collective-permute-start(s32[16,512]{1,0:T(8,128)S(1)} %add_select_fusion.1), channel_id=1, source_target_pairs={{0,16},{1,17},{2,18},{3,19},{4,20},{5,21},{6,22},{7,23},{8,24},{9,... | collective-permute-start | bytes 98312 | tf_op jit(solution)/shard_map/ppermute | solution.py:428
  32.8 1.6 %collective-permute-done.4 = s32[16,512]{1,0:T(8,128)S(1)} collective-permute-done((s32[16,512]{1,0:T(8,128)S(1)}, s32[16,512]{1,0:T(8,128)S(1)}, u32[]{:S(2)}, u32[]{:S(2)}) %collective-permute-start.4) | collective-permute-done | bytes 32800 | tf_op jit(solution)/shard_map/ppermute | solution.py:428
  34.4 0.1 copy.12
  34.5 0.2 copy.13
  34.7 0.6 pad.4.refs_1_
  35.3 0.0 copy-done
  35.3 0.9 slice_bitcast_fusion
  36.2 0.0 all-to-all-done
  36.2 0.0 copy-start.1
  36.3 7.1 %all-to-all-start.2 = ((bf16[32,8,1280]{2,1,0:T(8,128)(2,1)}), bf16[32,8,1280]{2,1,0:T(8,128)(2,1)S(1)}, u32[]{:S(2)}, u32[]{:S(2)}) async-start(bf16[32,8,1280]{2,1,0:T(8,128)(2,1)} %slice_bitcast_fusion), calls=%async_computation.2 | async-start | bytes 1310720 | tf_op jit(solution)/shard_map/all_to_all | solution.py:419
  43.3 0.0 copy-done.1
  43.3 19.0 %shard_map.104 = (bf16[256,1280]{1,0:T(8,128)(2,1)}, bf16[256,128]{1,0:T(8,128)(2,1)}) custom-call(bf16[256,1280]{1,0:T(8,128)(2,1)} %bitcast.19, bf16[256,128]{1,0:T(8,128)(2,1)} %pad.4.refs_1_, bf16[1280,640]{1,0:T(8,128)(2,1)} %refs_3_.3, bf16[3,640,640]{2,1,0:T(8,128)(2,1)} %refs_4_.3, bf16[640,1280]{1,0:T(8,128)(2,1)} %refs_5_.3, ...), custom_call_target="tpu_custom_call" | custom-call | flops 7549747200 | bytes 25165824 | tf_op jit(solution)/shard_map/pallas_call | solution.py:347
  62.3 0.0 all-to-all-done.2
  62.3 0.0 copy-start.2
  62.3 5.8 %all-to-all-start.1 = ((bf16[32,8,1280]{2,1,0:T(8,128)(2,1)}), bf16[32,8,1280]{2,1,0:T(8,128)(2,1)S(1)}, u32[]{:S(2)}, u32[]{:S(2)}) async-start(bf16[32,8,1280]{2,1,0:T(8,128)(2,1)} %bitcast.21), calls=%async_computation.1 | async-start | bytes 1310720 | tf_op jit(solution)/shard_map/all_to_all | solution.py:419
  68.2 0.0 copy-done.2
  68.2 19.1 %shard_map.105 = bf16[256,1408]{1,0:T(8,128)(2,1)} custom-call(bf16[256,1280]{1,0:T(8,128)(2,1)} %bitcast.20, bf16[256,128]{1,0:T(8,128)(2,1)} %pad.4.refs_1_, bf16[256,128]{1,0:T(8,128)(2,1)} %get-tuple-element.11.refs_2_, bf16[1280,640]{1,0:T(8,128)(2,1)} %refs_3_.3, bf16[3,640,640]{2,1,0:T(8,128)(2,1)} %refs_4_.3, bf16[640,1280]{1,0:T(8,128)(2,1)} %refs_5_.3, ...), custom_call_target="tpu_custom_call" | custom-call | flops 7549747200 | bytes 25165824 | tf_op jit(solution)/shard_map/pallas_call | solution.py:347
  87.3 0.0 all-to-all-done.1
  87.3 25.3 %all_to_all.20 = bf16[32,8,1408]{2,1,0:T(8,128)(2,1)S(1)} all-to-all(bf16[32,8,1408]{2,1,0:T(8,128)(2,1)} %bitcast.18), channel_id=1, replica_groups=mesh['coarse'=8,'fine'=4] {'coarse','fine'}, dimensions={0} | all-to-all | bytes 1441792 | tf_op jit(solution)/shard_map/all_to_all | solution.py:419
  112.6 1.6 %shard_map.106 = (bf16[512,1280]{1,0:T(8,128)(2,1)}, f32[4,128]{1,0:T(4,128)}) custom-call(bf16[256,1280]{1,0:T(8,128)(2,1)S(1)} %bitcast.17, bf16[256,1408]{1,0:T(8,128)(2,1)S(1)} %bitcast.16), custom_call_target="tpu_custom_call" | custom-call | tf_op jit(solution)/shard_map/pallas_call | solution.py:394
  (6 shorter events, 0.1 us)
Async XLA Ops:
  0.6 34.7 %copy-start = (bf16[512,1280]{1,0:T(8,128)(2,1)S(1)}, bf16[512,1280]{1,0:T(8,128)(2,1)}, u32[]{:S(2)}) copy-start(bf16[512,1280]{1,0:T(8,128)(2,1)} %param.9) | copy-start | bytes 3932164
  0.6 9.2 %copy-start.3 = (s32[512]{0:T(512)S(1)}, s32[512]{0:T(512)}, u32[]{:S(2)}) copy-start(s32[512]{0:T(512)} %param.10) | copy-start | bytes 6148
  2.7 33.5 %all-to-all-start = ((bf16[32,8,1280]{2,1,0:T(8,128)(2,1)}), bf16[32,8,1280]{2,1,0:T(8,128)(2,1)S(1)}, u32[]{:S(2)}, u32[]{:S(2)}) async-start(bf16[32,8,1280]{2,1,0:T(8,128)(2,1)} %slice_bitcast_fusion.1), calls=%async_computation | async-start | bytes 1310720 | tf_op jit(solution)/shard_map/all_to_all | solution.py:419
  9.8 10.9 %collective-permute-start = (s32[1,512]{1,0:T(1,128)S(1)}, s32[1,512]{1,0:T(1,128)S(1)}, u32[]{:S(2)}, u32[]{:S(2)}) collective-permute-start(s32[1,512]{1,0:T(1,128)S(1)} %bitcast.24), channel_id=1, source_target_pairs={{0,1},{1,0},{2,3},{3,2},{4,5},{5,4},{6,7},{7,6},{8,9},{9,8},{10,11... | collective-permute-start | bytes 6152 | tf_op jit(solution)/shard_map/ppermute | solution.py:428
  20.7 6.0 %collective-permute-start.1 = (s32[2,512]{1,0:T(2,128)S(1)}, s32[2,512]{1,0:T(2,128)S(1)}, u32[]{:S(2)}, u32[]{:S(2)}) collective-permute-start(s32[2,512]{1,0:T(2,128)S(1)} %add_select_fusion.4), channel_id=1, source_target_pairs={{0,2},{1,3},{2,0},{3,1},{4,6},{5,7},{6,4},{7,5},{8,10},{9,11},{10,... | collective-permute-start | bytes 12296 | tf_op jit(solution)/shard_map/ppermute | solution.py:428
  26.7 2.2 %collective-permute-start.2 = (s32[4,512]{1,0:T(4,128)S(1)}, s32[4,512]{1,0:T(4,128)S(1)}, u32[]{:S(2)}, u32[]{:S(2)}) collective-permute-start(s32[4,512]{1,0:T(4,128)S(1)} %add_select_fusion.3), channel_id=1, source_target_pairs={{0,4},{1,5},{2,6},{3,7},{4,0},{5,1},{6,2},{7,3},{8,12},{9,13},{10,... | collective-permute-start | bytes 24584 | tf_op jit(solution)/shard_map/ppermute | solution.py:428
  28.9 2.7 %collective-permute-start.3 = (s32[8,512]{1,0:T(8,128)S(1)}, s32[8,512]{1,0:T(8,128)S(1)}, u32[]{:S(2)}, u32[]{:S(2)}) collective-permute-start(s32[8,512]{1,0:T(8,128)S(1)} %add_select_fusion.2), channel_id=1, source_target_pairs={{0,8},{1,9},{2,10},{3,11},{4,12},{5,13},{6,14},{7,15},{8,0},{9,1},... | collective-permute-start | bytes 49160 | tf_op jit(solution)/shard_map/ppermute | solution.py:428
  31.6 2.8 %collective-permute-start.4 = (s32[16,512]{1,0:T(8,128)S(1)}, s32[16,512]{1,0:T(8,128)S(1)}, u32[]{:S(2)}, u32[]{:S(2)}) collective-permute-start(s32[16,512]{1,0:T(8,128)S(1)} %add_select_fusion.1), channel_id=1, source_target_pairs={{0,16},{1,17},{2,18},{3,19},{4,20},{5,21},{6,22},{7,23},{8,24},{9,... | collective-permute-start | bytes 98312 | tf_op jit(solution)/shard_map/ppermute | solution.py:428
  36.2 7.1 %copy-start.1 = (bf16[32,8,1280]{2,1,0:T(8,128)(2,1)}, bf16[32,8,1280]{2,1,0:T(8,128)(2,1)S(1)}, u32[]{:S(2)}) copy-start(bf16[32,8,1280]{2,1,0:T(8,128)(2,1)S(1)} %all-to-all-done) | copy-start | bytes 1966084
  36.3 26.1 %all-to-all-start.2 = ((bf16[32,8,1280]{2,1,0:T(8,128)(2,1)}), bf16[32,8,1280]{2,1,0:T(8,128)(2,1)S(1)}, u32[]{:S(2)}, u32[]{:S(2)}) async-start(bf16[32,8,1280]{2,1,0:T(8,128)(2,1)} %slice_bitcast_fusion), calls=%async_computation.2 | async-start | bytes 1310720 | tf_op jit(solution)/shard_map/all_to_all | solution.py:419
  62.3 5.9 %copy-start.2 = (bf16[32,8,1280]{2,1,0:T(8,128)(2,1)}, bf16[32,8,1280]{2,1,0:T(8,128)(2,1)S(1)}, u32[]{:S(2)}) copy-start(bf16[32,8,1280]{2,1,0:T(8,128)(2,1)S(1)} %all-to-all-done.2) | copy-start | bytes 1966084
  62.3 25.0 %all-to-all-start.1 = ((bf16[32,8,1280]{2,1,0:T(8,128)(2,1)}), bf16[32,8,1280]{2,1,0:T(8,128)(2,1)S(1)}, u32[]{:S(2)}, u32[]{:S(2)}) async-start(bf16[32,8,1280]{2,1,0:T(8,128)(2,1)} %bitcast.21), calls=%async_computation.1 | async-start | bytes 1310720 | tf_op jit(solution)/shard_map/all_to_all | solution.py:419

commit v5 on v3

--- a/solution.py
+++ b/solution.py
@@ -16,6 +16,7 @@
 CHUNKS = 2
 BLOCK = 256
 WHOLE_VMEM = 60 * 1024 * 1024
+KERNEL_VMEM = 52500 << 10
 SMALL_VMEM = 8 << 20
 
 
@@ -199,25 +200,24 @@
 
 def chain_kernel(near, far, block, chunk, last, *refs):
     refs = list(refs)
-    first_far = refs.pop(0)
-    x_far = refs.pop(0) if chunk else first_far
+    first_ref = refs.pop(0)
+    x_ref = refs.pop(0) if chunk else first_ref
     before_ref = refs.pop(0) if chunk else None
     *weights_far, dec_ref = refs[:7]
     refs = refs[7:]
     grad_ref = refs.pop(0)
     loss_ref = None if last else refs.pop(0)
-    x_ref, ws_in, wt_in, we_in, ws_out, wt_out, we_out, target_ref = refs[:8]
-    dec_pad, mid_a, mid_b, outer_in, carried = refs[8:13]
-    kept = [refs[start : start + 3] for start in range(13, 31, 3)]
+    ws_in, wt_in, we_in, ws_out, wt_out, we_out = refs[:6]
+    dec_pad, mid_a, mid_b, outer_in, carried = refs[6:11]
+    kept = [refs[start : start + 3] for start in range(11, 29, 3)]
     in_a, mid_kept_a, con_a, in_b, mid_kept_b, con_b = kept
-    sems = refs[31]
-    total, width = x_ref.shape
+    sems = refs[29]
+    total, width = x_ref.shape[0], ws_in.shape[0]
     wide, classes = pl.ds(0, width), dec_ref.shape[0]
     starts = range(0, total, block)
-    sources = [x_far.at[:, wide]] + weights_far + [first_far.at[:, pl.ds(width, LANES)]]
     copies = [
         pltpu.make_async_copy(source, target, sems.at[index])
-        for index, (source, target) in enumerate(zip(sources, refs[:8]))
+        for index, (source, target) in enumerate(zip(weights_far, refs[:6]))
     ]
     for copy in copies:
         copy.start()
@@ -249,16 +249,16 @@
             jnp.concatenate([taps[0], taps[1], taps[2]], axis=1),
         )
 
-    copies[0].wait()
-    copies[1].wait()
     for start in starts:
         rows = pl.ds(start, block)
         entry = activate(x_ref[rows, wide].astype(F32), in_a, rows)
+        if start == 0:
+            copies[0].wait()
         middle = activate(product(entry, ws_in[...]), mid_kept_a, rows)
         mid_a[pl.ds(start + near, block), :] = middle
     wrap(mid_a)
 
-    for copy in copies[2:5]:
+    for copy in copies[1:4]:
         copy.wait()
     for start in starts:
         rows = pl.ds(start, block)
@@ -269,7 +269,7 @@
         entry = activate(following.astype(F32), in_b, rows)
         mid_b[rows, :] = activate(product(entry, ws_out[...]), mid_kept_b, rows)
 
-    for copy in copies[5:]:
+    for copy in copies[4:]:
         copy.wait()
     for start in starts:
         rows = pl.ds(start, block)
@@ -281,7 +281,7 @@
         lane = lax.broadcasted_iota(jnp.int32, logits.shape, 1)
         exponent = jnp.where(lane < classes, jnp.exp(logits), 0.0)
         totals = jnp.sum(exponent, axis=-1, keepdims=True)
-        target = target_ref[rows, :].astype(F32)[:, chunk : chunk + 1]
+        target = first_ref[rows, pl.ds(width, LANES)].astype(F32)[:, chunk : chunk + 1]
         onehot = jnp.where(lane.astype(F32) == target, 1.0, 0.0)
         loss = jnp.log(totals) - jnp.sum(logits * onehot, axis=-1, keepdims=True)
         pieces = before_ref[rows, :].astype(F32) if chunk else jnp.zeros_like(logits)
@@ -345,12 +345,10 @@
     return pl.pallas_call(
         functools.partial(chain_kernel, near, far, block, chunk, last),
         out_shape=out_shape,
-        in_specs=[ANY] * (2 if chunk else 1) + [VMEM] * (1 if chunk else 0) + [ANY] * 6 + [VMEM],
+        in_specs=[VMEM] * (3 if chunk else 1) + [ANY] * 6 + [VMEM],
         out_specs=(VMEM,) * len(out_shape),
-        scratch_shapes=[pltpu.VMEM((count, width), BF)]
-        + [pltpu.VMEM(weight.shape, BF) for weight in weights[:6]]
+        scratch_shapes=[pltpu.VMEM(weight.shape, BF) for weight in weights[:6]]
         + [
-            pltpu.VMEM((count, LANES), BF),
             pltpu.VMEM((LANES, width), BF),
             pltpu.VMEM((padded, bottleneck), BF),
             pltpu.VMEM((padded, bottleneck), BF),
@@ -359,46 +357,65 @@
         ]
         + one_block
         + one_block
-        + [pltpu.SemaphoreType.DMA((8,))],
-        compiler_params=pltpu.CompilerParams(vmem_limit_bytes=WHOLE_VMEM),
+        + [pltpu.SemaphoreType.DMA((6,))],
+        compiler_params=pltpu.CompilerParams(vmem_limit_bytes=KERNEL_VMEM),
         cost_estimate=pl.CostEstimate(
             flops=count * 36 * width * bottleneck, bytes_accessed=24 << 20, transcendentals=0
         ),
     )(*operands)
 
 
-def pack_kernel(x_ref, target_ref, *refs):
-    outs, sems = refs[:-1], refs[-1]
-    part, width = outs[-1].shape
-    copies = []
-    for chunk, out in enumerate(outs):
-        source = x_ref.at[pl.ds(chunk * part, part), :]
-        copies.append(pltpu.make_async_copy(source, out.at[:, pl.ds(0, width)], sems.at[chunk]))
-        copies[-1].start()
+def pack_kernel(chunks, x_ref, target_ref, out_ref, sems):
+    part, width = out_ref.shape[0], x_ref.shape[1]
+    source = x_ref.at[pl.ds(0, part), :]
+    copy = pltpu.make_async_copy(source, out_ref.at[:, pl.ds(0, width)], sems.at[0])
+    copy.start()
     lane = lax.broadcasted_iota(jnp.int32, (LANES, LANES), 1)
     for start in range(0, part, LANES):
         tile = jnp.zeros((LANES, LANES), F32)
-        for chunk in range(len(outs)):
+        for chunk in range(chunks):
             row = target_ref[pl.ds((chunk * part + start) // LANES, 1), :].astype(F32)
             column = jnp.transpose(jnp.broadcast_to(row, (LANES, LANES)))
             tile = jnp.where(lane == chunk, column, tile)
-        outs[0][pl.ds(start, LANES), pl.ds(width, LANES)] = tile.astype(BF)
+        out_ref[pl.ds(start, LANES), pl.ds(width, LANES)] = tile.astype(BF)
+    copy.wait()
+
+
+def pack(activations, targets, chunks):
+    rows, width = activations.shape
+    return pl.pallas_call(
+        functools.partial(pack_kernel, chunks),
+        out_shape=jax.ShapeDtypeStruct((rows // chunks, width + LANES), BF),
+        in_specs=[ANY, VMEM],
+        out_specs=VMEM,
+        scratch_shapes=[pltpu.SemaphoreType.DMA((1,))],
+        compiler_params=pltpu.CompilerParams(vmem_limit_bytes=WHOLE_VMEM),
+    )(activations, targets.reshape(rows // LANES, LANES))
+
+
+def rest_kernel(x_ref, *refs):
+    outs, sems = refs[:-1], refs[-1]
+    part = outs[0].shape[0]
+    copies = [
+        pltpu.make_async_copy(x_ref.at[pl.ds((chunk + 1) * part, part), :], out, sems.at[chunk])
+        for chunk, out in enumerate(outs)
+    ]
+    for copy in copies:
+        copy.start()
     for copy in copies:
         copy.wait()
 
 
-def pack(activations, targets, chunks):
+def rest(activations, chunks):
     rows, width = activations.shape
-    part = rows // chunks
-    widths = [width + LANES] + [width] * (chunks - 1)
     return pl.pallas_call(
-        pack_kernel,
-        out_shape=tuple(jax.ShapeDtypeStruct((part, size), BF) for size in widths),
-        in_specs=[ANY, VMEM],
-        out_specs=(VMEM,) * chunks,
-        scratch_shapes=[pltpu.SemaphoreType.DMA((chunks,))],
+        rest_kernel,
+        out_shape=(jax.ShapeDtypeStruct((rows // chunks, width), BF),) * (chunks - 1),
+        in_specs=[ANY],
+        out_specs=(VMEM,) * (chunks - 1),
+        scratch_shapes=[pltpu.SemaphoreType.DMA((chunks - 1,))],
         compiler_params=pltpu.CompilerParams(vmem_limit_bytes=WHOLE_VMEM),
-    )(activations, targets.reshape(rows // LANES, LANES))
+    )(activations)
 
 
 def unpack_kernel(*refs):
@@ -453,7 +470,10 @@
         return moved.reshape(values.shape)
 
     there = []
-    for piece in pack(activations, targets, chunks):
+    pieces = [pack(activations, targets, chunks)]
+    if chunks > 1:
+        pieces += rest(activations, chunks)
+    for piece in pieces:
         there.append(spread(piece))
     losses = None
     homes = []

time: 103 us -> 99.5 us (0.966)
  blocking collectives: 51.9 us -> 23.2 us
  waiting for transfers between devices: 0.08 us -> 20.1 us
  starting transfers between devices: 8.93 us -> 15.3 us
  Pallas kernels: 40.8 us -> 39.6 us
    all_to_all x2 -> x1, blocking collectives: 51.9 us -> 23.2 us  [spread(): moved = lax.all_to_all(shaped, axes, 0, 0, tiled=True)]
    all_to_all x2 -> x3, waiting for transfers between devices: 0.08 us -> 20.1 us  [spread(): moved = lax.all_to_all(shaped, axes, 0, 0, tiled=True)]
    all_to_all x2 -> x3, starting transfers between devices: 8.93 us -> 15.3 us  [spread(): moved = lax.all_to_all(shaped, axes, 0, 0, tiled=True)]
    pallas_call x2, Pallas kernels: 36 us -> 33.4 us  [run_chains(): pl.pallas_call(functools.partial(chain_kernel, near, far, block, chunk, l...]
    pallas_call x1 -> x2, Pallas kernels: 3.06 us -> 4.58 us  [the longest x1 2.64 us: pack(): pl.pallas_call(functools.partial(pack_kernel, chunks), out_shape=jax.Shap...]
  transfers between devices with their start and end apart: 2 -> 3, of which waited for: 1 -> 3; matrix products, arithmetic and copies ran while one was open for 0% -> 0% of each run, Pallas kernels for 35% -> 36%
where the time goes in v5:
time: 99.5 us; the launch traced here: 99.1 us
  Pallas kernels  39.6 us (40%)
  blocking collectives  23.2 us (23%)
  waiting for transfers between devices  20.1 us (20%)
  starting transfers between devices  15.3 us (15%)
    pallas_call x2, Pallas kernels, run_chains(): pl.pallas_call(functools.partial(chain_kernel, near, far, block, chunk, l...  33.4 us
    all_to_all x1, blocking collectives, spread(): moved = lax.all_to_all(shaped, axes, 0, 0, tiled=True)  23.2 us
    all_to_all x3, waiting for transfers between devices, spread(): moved = lax.all_to_all(shaped, axes, 0, 0, tiled=True)  20.1 us
    all_to_all x3, starting transfers between devices, spread(): moved = lax.all_to_all(shaped, axes, 0, 0, tiled=True)  15.3 us
    pallas_call x1, Pallas kernels, pack(): pl.pallas_call(functools.partial(pack_kernel, chunks), out_shape=jax.Shap...  2.64 us
  transfers between devices with their start and end apart: 3, of which 3 were waited for; matrix products, arithmetic and copies ran while one was open for 0% of the time, Pallas kernels for 36%

profile of v5, /device:TPU:1, one launch (start us, length us, event | category | flops | bytes accessed | tf_op | source)
XLA Modules:
  0.0 99.1 jit_solution(1531181756051799252)
XLA Ops:
  0.6 2.6 %shard_map.104 = bf16[256,1408]{1,0:T(8,128)(2,1)} custom-call(bf16[512,1280]{1,0:T(8,128)(2,1)} %x_ref.3, s32[4,128]{1,0:T(4,128)} %bitcast.18), custom_call_target="tpu_custom_call" | custom-call | tf_op jit(solution)/shard_map/pallas_call | solution.py:386
  3.3 7.1 %all-to-all-start = ((bf16[32,8,1408]{2,1,0:T(8,128)(2,1)}), bf16[32,8,1408]{2,1,0:T(8,128)(2,1)S(1)}, u32[]{:S(2)}, u32[]{:S(2)}) async-start(bf16[32,8,1408]{2,1,0:T(8,128)(2,1)} %bitcast.16), calls=%async_computation | async-start | bytes 1441792 | tf_op jit(solution)/shard_map/all_to_all | solution.py:469
  10.4 0.0 copy-start
  10.4 1.9 %shard_map.106 = bf16[256,1280]{1,0:T(8,128)(2,1)} custom-call(bf16[512,1280]{1,0:T(8,128)(2,1)} %x_ref.3), custom_call_target="tpu_custom_call" | custom-call | tf_op jit(solution)/shard_map/pallas_call | solution.py:411
  12.3 17.5 %all-to-all-done = bf16[32,8,1408]{2,1,0:T(8,128)(2,1)S(1)} async-done(((bf16[32,8,1408]{2,1,0:T(8,128)(2,1)}), bf16[32,8,1408]{2,1,0:T(8,128)(2,1)S(1)}, u32[]{:S(2)}, u32[]{:S(2)}) %all-to-all-start) | async-done | bytes 720928 | tf_op jit(solution)/shard_map/all_to_all | solution.py:469
  29.8 3.2 %all-to-all-start.2 = ((bf16[32,8,1280]{2,1,0:T(8,128)(2,1)}), bf16[32,8,1280]{2,1,0:T(8,128)(2,1)S(1)}, u32[]{:S(2)}, u32[]{:S(2)}) async-start(bf16[32,8,1280]{2,1,0:T(8,128)(2,1)} %bitcast.17), calls=%async_computation.2 | async-start | bytes 1310720 | tf_op jit(solution)/shard_map/all_to_all | solution.py:469
  32.9 0.0 copy-done
  33.0 17.2 %shard_map.105 = (bf16[256,1280]{1,0:T(8,128)(2,1)}, bf16[256,128]{1,0:T(8,128)(2,1)S(1)}) custom-call(bf16[256,1408]{1,0:T(8,128)(2,1)S(1)} %bitcast.12, bf16[1280,640]{1,0:T(8,128)(2,1)} %refs_3_.3, bf16[3,640,640]{2,1,0:T(8,128)(2,1)} %refs_4_.3, bf16[640,1280]{1,0:T(8,128)(2,1)} %refs_5_.3, bf16[1280,640]{1,0:T(8,128)(2,1)} %refs_6_.3, ...), custom_call_target="tpu_custom_call" | custom-call | flops 7549747200 | bytes 25165824 | tf_op jit(solution)/shard_map/pallas_call | solution.py:345
  50.2 0.8 all-to-all-done.2
  51.0 5.0 %all-to-all-start.1 = ((bf16[32,8,1280]{2,1,0:T(8,128)(2,1)}), bf16[32,8,1280]{2,1,0:T(8,128)(2,1)S(1)}, u32[]{:S(2)}, u32[]{:S(2)}) async-start(bf16[32,8,1280]{2,1,0:T(8,128)(2,1)} %bitcast.3), calls=%async_computation.1 | async-start | bytes 1310720 | tf_op jit(solution)/shard_map/all_to_all | solution.py:469
  56.0 16.2 %shard_map.107 = bf16[256,1408]{1,0:T(8,128)(2,1)S(1)} custom-call(bf16[256,1408]{1,0:T(8,128)(2,1)S(1)} %bitcast.13, bf16[256,1280]{1,0:T(8,128)(2,1)S(1)} %bitcast.15, bf16[256,128]{1,0:T(8,128)(2,1)S(1)} %get-tuple-element.7.refs_2_, bf16[1280,640]{1,0:T(8,128)(2,1)} %refs_3_.3, bf16[3,640,640]{2,1,0:T(8,128)(2,1)} %refs_4_.3, bf16[640,1280]{1,0:T(8,128)(2,1)} %refs_5_.3, ...), custom_call_target="tpu_custom_call" | custom-call | flops 7549747200 | bytes 25165824 | tf_op jit(solution)/shard_map/pallas_call | solution.py:345
  72.2 1.9 %all-to-all-done.1 = bf16[32,8,1280]{2,1,0:T(8,128)(2,1)S(1)} async-done(((bf16[32,8,1280]{2,1,0:T(8,128)(2,1)}), bf16[32,8,1280]{2,1,0:T(8,128)(2,1)S(1)}, u32[]{:S(2)}, u32[]{:S(2)}) %all-to-all-start.1) | async-done | bytes 655392 | tf_op jit(solution)/shard_map/all_to_all | solution.py:469
  74.1 23.2 %all_to_all.20 = bf16[32,8,1408]{2,1,0:T(8,128)(2,1)S(1)} all-to-all(bf16[32,8,1408]{2,1,0:T(8,128)(2,1)S(1)} %bitcast.14), channel_id=1, replica_groups=mesh['coarse'=8,'fine'=4] {'coarse','fine'}, dimensions={0} | all-to-all | bytes 1441792 | tf_op jit(solution)/shard_map/all_to_all | solution.py:469
  97.3 1.6 %shard_map.108 = (bf16[512,1280]{1,0:T(8,128)(2,1)}, f32[4,128]{1,0:T(4,128)}) custom-call(bf16[256,1280]{1,0:T(8,128)(2,1)S(1)} %bitcast.11, bf16[256,1408]{1,0:T(8,128)(2,1)S(1)} %bitcast.10), custom_call_target="tpu_custom_call" | custom-call | tf_op jit(solution)/shard_map/pallas_call | solution.py:444
Async XLA Ops:
  3.3 26.5 %all-to-all-start = ((bf16[32,8,1408]{2,1,0:T(8,128)(2,1)}), bf16[32,8,1408]{2,1,0:T(8,128)(2,1)S(1)}, u32[]{:S(2)}, u32[]{:S(2)}) async-start(bf16[32,8,1408]{2,1,0:T(8,128)(2,1)} %bitcast.16), calls=%async_computation | async-start | bytes 1441792 | tf_op jit(solution)/shard_map/all_to_all | solution.py:469
  10.4 22.6 %copy-start = (bf16[5,1280]{1,0:T(8,128)(2,1)S(1)}, bf16[5,1280]{1,0:T(8,128)(2,1)}, u32[]{:S(2)}) copy-start(bf16[5,1280]{1,0:T(8,128)(2,1)} %refs_9_.1) | copy-start | bytes 38404
  29.8 21.2 %all-to-all-start.2 = ((bf16[32,8,1280]{2,1,0:T(8,128)(2,1)}), bf16[32,8,1280]{2,1,0:T(8,128)(2,1)S(1)}, u32[]{:S(2)}, u32[]{:S(2)}) async-start(bf16[32,8,1280]{2,1,0:T(8,128)(2,1)} %bitcast.17), calls=%async_computation.2 | async-start | bytes 1310720 | tf_op jit(solution)/shard_map/all_to_all | solution.py:469
  51.0 23.1 %all-to-all-start.1 = ((bf16[32,8,1280]{2,1,0:T(8,128)(2,1)}), bf16[32,8,1280]{2,1,0:T(8,128)(2,1)S(1)}, u32[]{:S(2)}, u32[]{:S(2)}) async-start(bf16[32,8,1280]{2,1,0:T(8,128)(2,1)} %bitcast.3), calls=%async_computation.1 | async-start | bytes 1310720 | tf_op jit(solution)/shard_map/all_to_all | solution.py:469

commit v6 on v5

--- a/solution.py
+++ b/solution.py
@@ -16,6 +16,7 @@
 CHUNKS = 2
 BLOCK = 256
 WHOLE_VMEM = 60 * 1024 * 1024
+PACK_STEPS = 4
 KERNEL_VMEM = 52500 << 10
 SMALL_VMEM = 8 << 20
 
@@ -243,6 +244,23 @@
             jnp.concatenate([behind, here, ahead], axis=1), taps[...].reshape(-1, taps.shape[2])
         )
 
+    meet = 2 * far % total == 0
+
+    def both_ends(taps):
+        return (taps[0].astype(F32) + taps[2].astype(F32)).astype(BF)
+
+    def far_conv(behind, here, ahead, taps):
+        if not meet:
+            return conv(behind, here, ahead, taps)
+        weight = jnp.concatenate([both_ends(taps), taps[1]])
+        return product(jnp.concatenate([behind, here], axis=1), weight)
+
+    def far_conv_back(behind, here, ahead, taps):
+        if not meet:
+            return conv_back(behind, here, ahead, taps)
+        weight = jnp.concatenate([both_ends(taps), taps[1]], axis=1)
+        return product_t(jnp.concatenate([ahead, here], axis=1), weight)
+
     def conv_back(behind, here, ahead, taps):
         return product_t(
             jnp.concatenate([ahead, here, behind], axis=1),
@@ -274,7 +292,7 @@
     for start in starts:
         rows = pl.ds(start, block)
         shifted = [far_rows(mid_b, start, shift) for shift in (-far, 0, far)]
-        closing = activate(conv(*shifted, wt_out), con_b, rows)
+        closing = activate(far_conv(*shifted, wt_out), con_b, rows)
         final = (outer_in[rows, :].astype(F32) + product(closing, we_out[...])).astype(BF)
         normal, factor = scaled_norm(final.astype(F32), 1.0)
         logits = product_t(normal.astype(BF), dec_pad[...])
@@ -302,7 +320,7 @@
     for start in starts:
         rows = pl.ds(start, block)
         shifted = [far_rows(mid_a, start, shift) for shift in (-far, 0, far)]
-        dmiddle = conv_back(*shifted, wt_out)
+        dmiddle = far_conv_back(*shifted, wt_out)
         dsqueezed = back(dmiddle, mid_kept_b, rows).astype(BF)
         upward = carried[rows, :] + back(product_t(dsqueezed, ws_out[...]), in_b, rows)
         carried[rows, :] = upward
@@ -365,11 +383,18 @@
     )(*operands)
 
 
-def pack_kernel(chunks, x_ref, target_ref, out_ref, sems):
-    part, width = out_ref.shape[0], x_ref.shape[1]
-    source = x_ref.at[pl.ds(0, part), :]
-    copy = pltpu.make_async_copy(source, out_ref.at[:, pl.ds(0, width)], sems.at[0])
-    copy.start()
+def pack_kernel(chunks, x_ref, target_ref, out_ref, buffer, in_sems, out_sems):
+    part, width = buffer.shape[0], x_ref.shape[1]
+    size = part // PACK_STEPS
+    arrivals, departures = [], []
+    for step in range(PACK_STEPS):
+        rows = pl.ds(step * size, size)
+        here = buffer.at[rows, pl.ds(0, width)]
+        arrivals.append(pltpu.make_async_copy(x_ref.at[rows, :], here, in_sems.at[step]))
+        departures.append(
+            pltpu.make_async_copy(buffer.at[rows, :], out_ref.at[rows, :], out_sems.at[step])
+        )
+        arrivals[-1].start()
     lane = lax.broadcasted_iota(jnp.int32, (LANES, LANES), 1)
     for start in range(0, part, LANES):
         tile = jnp.zeros((LANES, LANES), F32)
@@ -377,18 +402,27 @@
             row = target_ref[pl.ds((chunk * part + start) // LANES, 1), :].astype(F32)
             column = jnp.transpose(jnp.broadcast_to(row, (LANES, LANES)))
             tile = jnp.where(lane == chunk, column, tile)
-        out_ref[pl.ds(start, LANES), pl.ds(width, LANES)] = tile.astype(BF)
-    copy.wait()
+        buffer[pl.ds(start, LANES), pl.ds(width, LANES)] = tile.astype(BF)
+    for arrival, departure in zip(arrivals, departures):
+        arrival.wait()
+        departure.start()
+    for departure in departures:
+        departure.wait()
 
 
 def pack(activations, targets, chunks):
     rows, width = activations.shape
+    shape = (rows // chunks, width + LANES)
     return pl.pallas_call(
         functools.partial(pack_kernel, chunks),
-        out_shape=jax.ShapeDtypeStruct((rows // chunks, width + LANES), BF),
+        out_shape=jax.ShapeDtypeStruct(shape, BF),
         in_specs=[ANY, VMEM],
-        out_specs=VMEM,
-        scratch_shapes=[pltpu.SemaphoreType.DMA((1,))],
+        out_specs=ANY,
+        scratch_shapes=[
+            pltpu.VMEM(shape, BF),
+            pltpu.SemaphoreType.DMA((PACK_STEPS,)),
+            pltpu.SemaphoreType.DMA((PACK_STEPS,)),
+        ],
         compiler_params=pltpu.CompilerParams(vmem_limit_bytes=WHOLE_VMEM),
     )(activations, targets.reshape(rows // LANES, LANES))
 

time: 99.5 us -> 98.5 us (0.990)
  Pallas kernels: 39.6 us -> 38.6 us
  transfers between devices with their start and end apart: 3 -> 3, of which waited for: 3 -> 3; matrix products, arithmetic and copies ran while one was open for 0% -> 0% of each run, Pallas kernels for 36% -> 35%
where the time goes in v6:
time: 98.5 us; the launch traced here: 98.1 us
  Pallas kernels  38.6 us (39%)
  blocking collectives  22.8 us (23%)
  waiting for transfers between devices  21 us (21%)
  starting transfers between devices  14.8 us (15%)
    pallas_call x2, Pallas kernels, run_chains(): pl.pallas_call(functools.partial(chain_kernel, near, far, block, chunk, l...  32.5 us
    all_to_all x1, blocking collectives, spread(): moved = lax.all_to_all(shaped, axes, 0, 0, tiled=True)  22.8 us
    all_to_all x3, waiting for transfers between devices, spread(): moved = lax.all_to_all(shaped, axes, 0, 0, tiled=True)  21 us
    all_to_all x3, starting transfers between devices, spread(): moved = lax.all_to_all(shaped, axes, 0, 0, tiled=True)  14.8 us
    pallas_call x1, Pallas kernels, pack(): pl.pallas_call(functools.partial(pack_kernel, chunks), out_shape=jax.Shap...  2.57 us
  transfers between devices with their start and end apart: 3, of which 3 were waited for; matrix products, arithmetic and copies ran while one was open for 0% of the time, Pallas kernels for 35%

profile of v6, /device:TPU:1, one launch (start us, length us, event | category | flops | bytes accessed | tf_op | source)
XLA Modules:
  0.0 98.1 jit_solution(13991161710625976966)
XLA Ops:
  0.6 2.6 %shard_map.104 = bf16[256,1408]{1,0:T(8,128)(2,1)} custom-call(bf16[512,1280]{1,0:T(8,128)(2,1)} %x_ref.3, s32[4,128]{1,0:T(4,128)} %bitcast.18), custom_call_target="tpu_custom_call" | custom-call | tf_op jit(solution)/shard_map/pallas_call | solution.py:416
  3.2 7.1 %all-to-all-start = ((bf16[32,8,1408]{2,1,0:T(8,128)(2,1)}), bf16[32,8,1408]{2,1,0:T(8,128)(2,1)S(1)}, u32[]{:S(2)}, u32[]{:S(2)}) async-start(bf16[32,8,1408]{2,1,0:T(8,128)(2,1)} %bitcast.16), calls=%async_computation | async-start | bytes 1441792 | tf_op jit(solution)/shard_map/all_to_all | solution.py:503
  10.3 0.0 copy-start
  10.3 1.9 %shard_map.106 = bf16[256,1280]{1,0:T(8,128)(2,1)} custom-call(bf16[512,1280]{1,0:T(8,128)(2,1)} %x_ref.3), custom_call_target="tpu_custom_call" | custom-call | tf_op jit(solution)/shard_map/pallas_call | solution.py:445
  12.3 17.5 %all-to-all-done = bf16[32,8,1408]{2,1,0:T(8,128)(2,1)S(1)} async-done(((bf16[32,8,1408]{2,1,0:T(8,128)(2,1)}), bf16[32,8,1408]{2,1,0:T(8,128)(2,1)S(1)}, u32[]{:S(2)}, u32[]{:S(2)}) %all-to-all-start) | async-done | bytes 720928 | tf_op jit(solution)/shard_map/all_to_all | solution.py:503
  29.7 3.2 %all-to-all-start.2 = ((bf16[32,8,1280]{2,1,0:T(8,128)(2,1)}), bf16[32,8,1280]{2,1,0:T(8,128)(2,1)S(1)}, u32[]{:S(2)}, u32[]{:S(2)}) async-start(bf16[32,8,1280]{2,1,0:T(8,128)(2,1)} %bitcast.17), calls=%async_computation.2 | async-start | bytes 1310720 | tf_op jit(solution)/shard_map/all_to_all | solution.py:503
  32.9 0.0 copy-done
  32.9 16.7 %shard_map.105 = (bf16[256,1280]{1,0:T(8,128)(2,1)}, bf16[256,128]{1,0:T(8,128)(2,1)S(1)}) custom-call(bf16[256,1408]{1,0:T(8,128)(2,1)S(1)} %bitcast.12, bf16[1280,640]{1,0:T(8,128)(2,1)} %refs_3_.3, bf16[3,640,640]{2,1,0:T(8,128)(2,1)} %refs_4_.3, bf16[640,1280]{1,0:T(8,128)(2,1)} %refs_5_.3, bf16[1280,640]{1,0:T(8,128)(2,1)} %refs_6_.3, ...), custom_call_target="tpu_custom_call" | custom-call | flops 7549747200 | bytes 25165824 | tf_op jit(solution)/shard_map/pallas_call | solution.py:363
  49.6 1.3 %all-to-all-done.2 = bf16[32,8,1280]{2,1,0:T(8,128)(2,1)S(1)} async-done(((bf16[32,8,1280]{2,1,0:T(8,128)(2,1)}), bf16[32,8,1280]{2,1,0:T(8,128)(2,1)S(1)}, u32[]{:S(2)}, u32[]{:S(2)}) %all-to-all-start.2) | async-done | bytes 655392 | tf_op jit(solution)/shard_map/all_to_all | solution.py:503
  50.9 4.6 %all-to-all-start.1 = ((bf16[32,8,1280]{2,1,0:T(8,128)(2,1)}), bf16[32,8,1280]{2,1,0:T(8,128)(2,1)S(1)}, u32[]{:S(2)}, u32[]{:S(2)}) async-start(bf16[32,8,1280]{2,1,0:T(8,128)(2,1)} %bitcast.3), calls=%async_computation.1 | async-start | bytes 1310720 | tf_op jit(solution)/shard_map/all_to_all | solution.py:503
  55.5 15.7 %shard_map.107 = bf16[256,1408]{1,0:T(8,128)(2,1)S(1)} custom-call(bf16[256,1408]{1,0:T(8,128)(2,1)S(1)} %bitcast.13, bf16[256,1280]{1,0:T(8,128)(2,1)S(1)} %bitcast.15, bf16[256,128]{1,0:T(8,128)(2,1)S(1)} %get-tuple-element.7.refs_2_, bf16[1280,640]{1,0:T(8,128)(2,1)} %refs_3_.3, bf16[3,640,640]{2,1,0:T(8,128)(2,1)} %refs_4_.3, bf16[640,1280]{1,0:T(8,128)(2,1)} %refs_5_.3, ...), custom_call_target="tpu_custom_call" | custom-call | flops 7549747200 | bytes 25165824 | tf_op jit(solution)/shard_map/pallas_call | solution.py:363
  71.2 2.3 %all-to-all-done.1 = bf16[32,8,1280]{2,1,0:T(8,128)(2,1)S(1)} async-done(((bf16[32,8,1280]{2,1,0:T(8,128)(2,1)}), bf16[32,8,1280]{2,1,0:T(8,128)(2,1)S(1)}, u32[]{:S(2)}, u32[]{:S(2)}) %all-to-all-start.1) | async-done | bytes 655392 | tf_op jit(solution)/shard_map/all_to_all | solution.py:503
  73.5 22.8 %all_to_all.20 = bf16[32,8,1408]{2,1,0:T(8,128)(2,1)S(1)} all-to-all(bf16[32,8,1408]{2,1,0:T(8,128)(2,1)S(1)} %bitcast.14), channel_id=1, replica_groups=mesh['coarse'=8,'fine'=4] {'coarse','fine'}, dimensions={0} | all-to-all | bytes 1441792 | tf_op jit(solution)/shard_map/all_to_all | solution.py:503
  96.3 1.6 %shard_map.108 = (bf16[512,1280]{1,0:T(8,128)(2,1)}, f32[4,128]{1,0:T(4,128)}) custom-call(bf16[256,1280]{1,0:T(8,128)(2,1)S(1)} %bitcast.11, bf16[256,1408]{1,0:T(8,128)(2,1)S(1)} %bitcast.10), custom_call_target="tpu_custom_call" | custom-call | tf_op jit(solution)/shard_map/pallas_call | solution.py:478
Async XLA Ops:
  3.2 26.5 %all-to-all-start = ((bf16[32,8,1408]{2,1,0:T(8,128)(2,1)}), bf16[32,8,1408]{2,1,0:T(8,128)(2,1)S(1)}, u32[]{:S(2)}, u32[]{:S(2)}) async-start(bf16[32,8,1408]{2,1,0:T(8,128)(2,1)} %bitcast.16), calls=%async_computation | async-start | bytes 1441792 | tf_op jit(solution)/shard_map/all_to_all | solution.py:503
  10.3 22.6 %copy-start = (bf16[5,1280]{1,0:T(8,128)(2,1)S(1)}, bf16[5,1280]{1,0:T(8,128)(2,1)}, u32[]{:S(2)}) copy-start(bf16[5,1280]{1,0:T(8,128)(2,1)} %refs_9_.1) | copy-start | bytes 38404
  29.7 21.2 %all-to-all-start.2 = ((bf16[32,8,1280]{2,1,0:T(8,128)(2,1)}), bf16[32,8,1280]{2,1,0:T(8,128)(2,1)S(1)}, u32[]{:S(2)}, u32[]{:S(2)}) async-start(bf16[32,8,1280]{2,1,0:T(8,128)(2,1)} %bitcast.17), calls=%async_computation.2 | async-start | bytes 1310720 | tf_op jit(solution)/shard_map/all_to_all | solution.py:503
  50.9 22.6 %all-to-all-start.1 = ((bf16[32,8,1280]{2,1,0:T(8,128)(2,1)}), bf16[32,8,1280]{2,1,0:T(8,128)(2,1)S(1)}, u32[]{:S(2)}, u32[]{:S(2)}) async-start(bf16[32,8,1280]{2,1,0:T(8,128)(2,1)} %bitcast.3), calls=%async_computation.1 | async-start | bytes 1310720 | tf_op jit(solution)/shard_map/all_to_all | solution.py:503

commit v7 on v6

--- a/solution.py
+++ b/solution.py
@@ -383,7 +383,9 @@
     )(*operands)
 
 
-def pack_kernel(chunks, x_ref, target_ref, out_ref, buffer, in_sems, out_sems):
+def pack_kernel(chunks, x_ref, target_far, out_ref, target_ref, buffer, in_sems, out_sems):
+    target_copy = pltpu.make_async_copy(target_far, target_ref, in_sems.at[PACK_STEPS])
+    target_copy.start()
     part, width = buffer.shape[0], x_ref.shape[1]
     size = part // PACK_STEPS
     arrivals, departures = [], []
@@ -395,6 +397,7 @@
             pltpu.make_async_copy(buffer.at[rows, :], out_ref.at[rows, :], out_sems.at[step])
         )
         arrivals[-1].start()
+    target_copy.wait()
     lane = lax.broadcasted_iota(jnp.int32, (LANES, LANES), 1)
     for start in range(0, part, LANES):
         tile = jnp.zeros((LANES, LANES), F32)
@@ -416,11 +419,12 @@
     return pl.pallas_call(
         functools.partial(pack_kernel, chunks),
         out_shape=jax.ShapeDtypeStruct(shape, BF),
-        in_specs=[ANY, VMEM],
+        in_specs=[ANY, ANY],
         out_specs=ANY,
         scratch_shapes=[
+            pltpu.VMEM((rows // LANES, LANES), targets.dtype),
             pltpu.VMEM(shape, BF),
-            pltpu.SemaphoreType.DMA((PACK_STEPS,)),
+            pltpu.SemaphoreType.DMA((PACK_STEPS + 1,)),
             pltpu.SemaphoreType.DMA((PACK_STEPS,)),
         ],
         compiler_params=pltpu.CompilerParams(vmem_limit_bytes=WHOLE_VMEM),

time: 98.5 us -> 97.9 us (level)
  no operation moved by 1% of the time
where the time goes in v7:
time: 97.9 us; the launch traced here: 97.5 us
  Pallas kernels  37.9 us (39%)
  blocking collectives  22.8 us (23%)
  waiting for transfers between devices  21 us (21%)
  starting transfers between devices  14.8 us (15%)
    pallas_call x2, Pallas kernels, run_chains(): pl.pallas_call(functools.partial(chain_kernel, near, far, block, chunk, l...  32.4 us
    all_to_all x1, blocking collectives, spread(): moved = lax.all_to_all(shaped, axes, 0, 0, tiled=True)  22.8 us
    all_to_all x3, waiting for transfers between devices, spread(): moved = lax.all_to_all(shaped, axes, 0, 0, tiled=True)  21 us
    all_to_all x3, starting transfers between devices, spread(): moved = lax.all_to_all(shaped, axes, 0, 0, tiled=True)  14.8 us
  transfers between devices with their start and end apart: 3, of which 3 were waited for; matrix products, arithmetic and copies ran while one was open for 0% of the time, Pallas kernels for 35%

profile of v7, /device:TPU:1, one launch (start us, length us, event | category | flops | bytes accessed | tf_op | source)
XLA Modules:
  0.0 97.5 jit_solution(1377094738594425682)
XLA Ops:
  0.6 1.9 %shard_map.104 = bf16[256,1408]{1,0:T(8,128)(2,1)} custom-call(bf16[512,1280]{1,0:T(8,128)(2,1)} %x_ref.3, s32[4,128]{1,0:T(4,128)} %bitcast.18), custom_call_target="tpu_custom_call" | custom-call | tf_op jit(solution)/shard_map/pallas_call | solution.py:419
  2.6 7.1 %all-to-all-start = ((bf16[32,8,1408]{2,1,0:T(8,128)(2,1)}), bf16[32,8,1408]{2,1,0:T(8,128)(2,1)S(1)}, u32[]{:S(2)}, u32[]{:S(2)}) async-start(bf16[32,8,1408]{2,1,0:T(8,128)(2,1)} %bitcast.16), calls=%async_computation | async-start | bytes 1441792 | tf_op jit(solution)/shard_map/all_to_all | solution.py:507
  9.7 0.0 copy-start
  9.7 1.9 %shard_map.106 = bf16[256,1280]{1,0:T(8,128)(2,1)} custom-call(bf16[512,1280]{1,0:T(8,128)(2,1)} %x_ref.3), custom_call_target="tpu_custom_call" | custom-call | tf_op jit(solution)/shard_map/pallas_call | solution.py:449
  11.6 17.5 %all-to-all-done = bf16[32,8,1408]{2,1,0:T(8,128)(2,1)S(1)} async-done(((bf16[32,8,1408]{2,1,0:T(8,128)(2,1)}), bf16[32,8,1408]{2,1,0:T(8,128)(2,1)S(1)}, u32[]{:S(2)}, u32[]{:S(2)}) %all-to-all-start) | async-done | bytes 720928 | tf_op jit(solution)/shard_map/all_to_all | solution.py:507
  29.1 3.2 %all-to-all-start.2 = ((bf16[32,8,1280]{2,1,0:T(8,128)(2,1)}), bf16[32,8,1280]{2,1,0:T(8,128)(2,1)S(1)}, u32[]{:S(2)}, u32[]{:S(2)}) async-start(bf16[32,8,1280]{2,1,0:T(8,128)(2,1)} %bitcast.17), calls=%async_computation.2 | async-start | bytes 1310720 | tf_op jit(solution)/shard_map/all_to_all | solution.py:507
  32.2 0.0 copy-done
  32.2 16.7 %shard_map.105 = (bf16[256,1280]{1,0:T(8,128)(2,1)}, bf16[256,128]{1,0:T(8,128)(2,1)S(1)}) custom-call(bf16[256,1408]{1,0:T(8,128)(2,1)S(1)} %bitcast.12, bf16[1280,640]{1,0:T(8,128)(2,1)} %refs_3_.3, bf16[3,640,640]{2,1,0:T(8,128)(2,1)} %refs_4_.3, bf16[640,1280]{1,0:T(8,128)(2,1)} %refs_5_.3, bf16[1280,640]{1,0:T(8,128)(2,1)} %refs_6_.3, ...), custom_call_target="tpu_custom_call" | custom-call | flops 7549747200 | bytes 25165824 | tf_op jit(solution)/shard_map/pallas_call | solution.py:363
  49.0 1.3 %all-to-all-done.2 = bf16[32,8,1280]{2,1,0:T(8,128)(2,1)S(1)} async-done(((bf16[32,8,1280]{2,1,0:T(8,128)(2,1)}), bf16[32,8,1280]{2,1,0:T(8,128)(2,1)S(1)}, u32[]{:S(2)}, u32[]{:S(2)}) %all-to-all-start.2) | async-done | bytes 655392 | tf_op jit(solution)/shard_map/all_to_all | solution.py:507
  50.3 4.6 %all-to-all-start.1 = ((bf16[32,8,1280]{2,1,0:T(8,128)(2,1)}), bf16[32,8,1280]{2,1,0:T(8,128)(2,1)S(1)}, u32[]{:S(2)}, u32[]{:S(2)}) async-start(bf16[32,8,1280]{2,1,0:T(8,128)(2,1)} %bitcast.3), calls=%async_computation.1 | async-start | bytes 1310720 | tf_op jit(solution)/shard_map/all_to_all | solution.py:507
  54.9 15.7 %shard_map.107 = bf16[256,1408]{1,0:T(8,128)(2,1)S(1)} custom-call(bf16[256,1408]{1,0:T(8,128)(2,1)S(1)} %bitcast.13, bf16[256,1280]{1,0:T(8,128)(2,1)S(1)} %bitcast.15, bf16[256,128]{1,0:T(8,128)(2,1)S(1)} %get-tuple-element.7.refs_2_, bf16[1280,640]{1,0:T(8,128)(2,1)} %refs_3_.3, bf16[3,640,640]{2,1,0:T(8,128)(2,1)} %refs_4_.3, bf16[640,1280]{1,0:T(8,128)(2,1)} %refs_5_.3, ...), custom_call_target="tpu_custom_call" | custom-call | flops 7549747200 | bytes 25165824 | tf_op jit(solution)/shard_map/pallas_call | solution.py:363
  70.6 2.3 %all-to-all-done.1 = bf16[32,8,1280]{2,1,0:T(8,128)(2,1)S(1)} async-done(((bf16[32,8,1280]{2,1,0:T(8,128)(2,1)}), bf16[32,8,1280]{2,1,0:T(8,128)(2,1)S(1)}, u32[]{:S(2)}, u32[]{:S(2)}) %all-to-all-start.1) | async-done | bytes 655392 | tf_op jit(solution)/shard_map/all_to_all | solution.py:507
  72.9 22.8 %all_to_all.20 = bf16[32,8,1408]{2,1,0:T(8,128)(2,1)S(1)} all-to-all(bf16[32,8,1408]{2,1,0:T(8,128)(2,1)S(1)} %bitcast.14), channel_id=1, replica_groups=mesh['coarse'=8,'fine'=4] {'coarse','fine'}, dimensions={0} | all-to-all | bytes 1441792 | tf_op jit(solution)/shard_map/all_to_all | solution.py:507
  95.6 1.6 %shard_map.108 = (bf16[512,1280]{1,0:T(8,128)(2,1)}, f32[4,128]{1,0:T(4,128)}) custom-call(bf16[256,1280]{1,0:T(8,128)(2,1)S(1)} %bitcast.11, bf16[256,1408]{1,0:T(8,128)(2,1)S(1)} %bitcast.10), custom_call_target="tpu_custom_call" | custom-call | tf_op jit(solution)/shard_map/pallas_call | solution.py:482
Async XLA Ops:
  2.6 26.5 %all-to-all-start = ((bf16[32,8,1408]{2,1,0:T(8,128)(2,1)}), bf16[32,8,1408]{2,1,0:T(8,128)(2,1)S(1)}, u32[]{:S(2)}, u32[]{:S(2)}) async-start(bf16[32,8,1408]{2,1,0:T(8,128)(2,1)} %bitcast.16), calls=%async_computation | async-start | bytes 1441792 | tf_op jit(solution)/shard_map/all_to_all | solution.py:507
  9.7 22.6 %copy-start = (bf16[5,1280]{1,0:T(8,128)(2,1)S(1)}, bf16[5,1280]{1,0:T(8,128)(2,1)}, u32[]{:S(2)}) copy-start(bf16[5,1280]{1,0:T(8,128)(2,1)} %refs_9_.1) | copy-start | bytes 38404
  29.1 21.2 %all-to-all-start.2 = ((bf16[32,8,1280]{2,1,0:T(8,128)(2,1)}), bf16[32,8,1280]{2,1,0:T(8,128)(2,1)S(1)}, u32[]{:S(2)}, u32[]{:S(2)}) async-start(bf16[32,8,1280]{2,1,0:T(8,128)(2,1)} %bitcast.17), calls=%async_computation.2 | async-start | bytes 1310720 | tf_op jit(solution)/shard_map/all_to_all | solution.py:507
  50.3 22.6 %all-to-all-start.1 = ((bf16[32,8,1280]{2,1,0:T(8,128)(2,1)}), bf16[32,8,1280]{2,1,0:T(8,128)(2,1)S(1)}, u32[]{:S(2)}, u32[]{:S(2)}) async-start(bf16[32,8,1280]{2,1,0:T(8,128)(2,1)} %bitcast.3), calls=%async_computation.1 | async-start | bytes 1310720 | tf_op jit(solution)/shard_map/all_to_all | solution.py:507

commit v8 on v7

--- a/solution.py
+++ b/solution.py
@@ -457,7 +457,7 @@
 
 
 def unpack_kernel(*refs):
-    *pieces, out_ref, loss_ref, sems = refs
+    *pieces, out_ref, loss_far, loss_ref, sems = refs
     part, width = pieces[-1].shape[0], out_ref.shape[1]
     copies = []
     for chunk, piece in enumerate(pieces):
@@ -468,10 +468,11 @@
         tile = pieces[-1][pl.ds(start, LANES), pl.ds(width, LANES)].astype(F32)
         flat = jnp.transpose(tile)
         for chunk in range(len(pieces)):
-            lines = [flat[chunk * PIECES + part : chunk * PIECES + part + 1] for part in range(PIECES)]
-            loss_ref[pl.ds((chunk * pieces[-1].shape[0] + start) // LANES, 1), :] = sum(
-                lines[1:], lines[0]
-            )
+            first = chunk * PIECES
+            lines = [flat[first + index : first + index + 1] for index in range(PIECES)]
+            loss_ref[pl.ds((chunk * part + start) // LANES, 1), :] = sum(lines[1:], lines[0])
+    copies.append(pltpu.make_async_copy(loss_ref, loss_far, sems.at[len(pieces)]))
+    copies[-1].start()
     for copy in copies:
         copy.wait()
 
@@ -486,8 +487,11 @@
             jax.ShapeDtypeStruct((rows // LANES, LANES), F32),
         ),
         in_specs=[VMEM] * chunks,
-        out_specs=(ANY, VMEM),
-        scratch_shapes=[pltpu.SemaphoreType.DMA((chunks,))],
+        out_specs=(ANY, ANY),
+        scratch_shapes=[
+            pltpu.VMEM((rows // LANES, LANES), F32),
+            pltpu.SemaphoreType.DMA((chunks + 1,)),
+        ],
         compiler_params=pltpu.CompilerParams(vmem_limit_bytes=SMALL_VMEM),
     )(*homes)
     return (result, losses.reshape(rows))

time: 97.9 us -> 97.3 us (level)
  no operation moved by 1% of the time
where the time goes in v8:
time: 97.3 us; the launch traced here: 96.9 us
  Pallas kernels  37.4 us (38%)
  blocking collectives  22.8 us (23%)
  waiting for transfers between devices  21 us (22%)
  starting transfers between devices  14.8 us (15%)
    pallas_call x2, Pallas kernels, run_chains(): pl.pallas_call(functools.partial(chain_kernel, near, far, block, chunk, l...  32.4 us
    all_to_all x1, blocking collectives, spread(): moved = lax.all_to_all(shaped, axes, 0, 0, tiled=True)  22.8 us
    all_to_all x3, waiting for transfers between devices, spread(): moved = lax.all_to_all(shaped, axes, 0, 0, tiled=True)  21 us
    all_to_all x3, starting transfers between devices, spread(): moved = lax.all_to_all(shaped, axes, 0, 0, tiled=True)  14.8 us
  transfers between devices with their start and end apart: 3, of which 3 were waited for; matrix products, arithmetic and copies ran while one was open for 0% of the time, Pallas kernels for 35%

profile of v8, /device:TPU:1, one launch (start us, length us, event | category | flops | bytes accessed | tf_op | source)
XLA Modules:
  0.0 96.9 jit_solution(3810925417074154386)
XLA Ops:
  0.6 1.9 %shard_map.104 = bf16[256,1408]{1,0:T(8,128)(2,1)} custom-call(bf16[512,1280]{1,0:T(8,128)(2,1)} %x_ref.3, s32[4,128]{1,0:T(4,128)} %bitcast.18), custom_call_target="tpu_custom_call" | custom-call | tf_op jit(solution)/shard_map/pallas_call | solution.py:419
  2.6 7.1 %all-to-all-start = ((bf16[32,8,1408]{2,1,0:T(8,128)(2,1)}), bf16[32,8,1408]{2,1,0:T(8,128)(2,1)S(1)}, u32[]{:S(2)}, u32[]{:S(2)}) async-start(bf16[32,8,1408]{2,1,0:T(8,128)(2,1)} %bitcast.16), calls=%async_computation | async-start | bytes 1441792 | tf_op jit(solution)/shard_map/all_to_all | solution.py:511
  9.7 0.0 copy-start
  9.7 1.9 %shard_map.106 = bf16[256,1280]{1,0:T(8,128)(2,1)} custom-call(bf16[512,1280]{1,0:T(8,128)(2,1)} %x_ref.3), custom_call_target="tpu_custom_call" | custom-call | tf_op jit(solution)/shard_map/pallas_call | solution.py:449
  11.6 17.5 %all-to-all-done = bf16[32,8,1408]{2,1,0:T(8,128)(2,1)S(1)} async-done(((bf16[32,8,1408]{2,1,0:T(8,128)(2,1)}), bf16[32,8,1408]{2,1,0:T(8,128)(2,1)S(1)}, u32[]{:S(2)}, u32[]{:S(2)}) %all-to-all-start) | async-done | bytes 720928 | tf_op jit(solution)/shard_map/all_to_all | solution.py:511
  29.1 3.2 %all-to-all-start.2 = ((bf16[32,8,1280]{2,1,0:T(8,128)(2,1)}), bf16[32,8,1280]{2,1,0:T(8,128)(2,1)S(1)}, u32[]{:S(2)}, u32[]{:S(2)}) async-start(bf16[32,8,1280]{2,1,0:T(8,128)(2,1)} %bitcast.17), calls=%async_computation.2 | async-start | bytes 1310720 | tf_op jit(solution)/shard_map/all_to_all | solution.py:511
  32.2 0.0 copy-done
  32.2 16.7 %shard_map.105 = (bf16[256,1280]{1,0:T(8,128)(2,1)}, bf16[256,128]{1,0:T(8,128)(2,1)S(1)}) custom-call(bf16[256,1408]{1,0:T(8,128)(2,1)S(1)} %bitcast.12, bf16[1280,640]{1,0:T(8,128)(2,1)} %refs_3_.3, bf16[3,640,640]{2,1,0:T(8,128)(2,1)} %refs_4_.3, bf16[640,1280]{1,0:T(8,128)(2,1)} %refs_5_.3, bf16[1280,640]{1,0:T(8,128)(2,1)} %refs_6_.3, ...), custom_call_target="tpu_custom_call" | custom-call | flops 7549747200 | bytes 25165824 | tf_op jit(solution)/shard_map/pallas_call | solution.py:363
  49.0 1.3 %all-to-all-done.2 = bf16[32,8,1280]{2,1,0:T(8,128)(2,1)S(1)} async-done(((bf16[32,8,1280]{2,1,0:T(8,128)(2,1)}), bf16[32,8,1280]{2,1,0:T(8,128)(2,1)S(1)}, u32[]{:S(2)}, u32[]{:S(2)}) %all-to-all-start.2) | async-done | bytes 655392 | tf_op jit(solution)/shard_map/all_to_all | solution.py:511
  50.3 4.6 %all-to-all-start.1 = ((bf16[32,8,1280]{2,1,0:T(8,128)(2,1)}), bf16[32,8,1280]{2,1,0:T(8,128)(2,1)S(1)}, u32[]{:S(2)}, u32[]{:S(2)}) async-start(bf16[32,8,1280]{2,1,0:T(8,128)(2,1)} %bitcast.3), calls=%async_computation.1 | async-start | bytes 1310720 | tf_op jit(solution)/shard_map/all_to_all | solution.py:511
  54.9 15.7 %shard_map.107 = bf16[256,1408]{1,0:T(8,128)(2,1)S(1)} custom-call(bf16[256,1408]{1,0:T(8,128)(2,1)S(1)} %bitcast.13, bf16[256,1280]{1,0:T(8,128)(2,1)S(1)} %bitcast.15, bf16[256,128]{1,0:T(8,128)(2,1)S(1)} %get-tuple-element.7.refs_2_, bf16[1280,640]{1,0:T(8,128)(2,1)} %refs_3_.3, bf16[3,640,640]{2,1,0:T(8,128)(2,1)} %refs_4_.3, bf16[640,1280]{1,0:T(8,128)(2,1)} %refs_5_.3, ...), custom_call_target="tpu_custom_call" | custom-call | flops 7549747200 | bytes 25165824 | tf_op jit(solution)/shard_map/pallas_call | solution.py:363
  70.6 2.3 %all-to-all-done.1 = bf16[32,8,1280]{2,1,0:T(8,128)(2,1)S(1)} async-done(((bf16[32,8,1280]{2,1,0:T(8,128)(2,1)}), bf16[32,8,1280]{2,1,0:T(8,128)(2,1)S(1)}, u32[]{:S(2)}, u32[]{:S(2)}) %all-to-all-start.1) | async-done | bytes 655392 | tf_op jit(solution)/shard_map/all_to_all | solution.py:511
  72.9 22.8 %all_to_all.20 = bf16[32,8,1408]{2,1,0:T(8,128)(2,1)S(1)} all-to-all(bf16[32,8,1408]{2,1,0:T(8,128)(2,1)S(1)} %bitcast.14), channel_id=1, replica_groups=mesh['coarse'=8,'fine'=4] {'coarse','fine'}, dimensions={0} | all-to-all | bytes 1441792 | tf_op jit(solution)/shard_map/all_to_all | solution.py:511
  95.6 1.1 %shard_map.108 = (bf16[512,1280]{1,0:T(8,128)(2,1)}, f32[4,128]{1,0:T(4,128)}) custom-call(bf16[256,1280]{1,0:T(8,128)(2,1)S(1)} %bitcast.11, bf16[256,1408]{1,0:T(8,128)(2,1)S(1)} %bitcast.10), custom_call_target="tpu_custom_call" | custom-call | tf_op jit(solution)/shard_map/pallas_call | solution.py:483
Async XLA Ops:
  2.6 26.5 %all-to-all-start = ((bf16[32,8,1408]{2,1,0:T(8,128)(2,1)}), bf16[32,8,1408]{2,1,0:T(8,128)(2,1)S(1)}, u32[]{:S(2)}, u32[]{:S(2)}) async-start(bf16[32,8,1408]{2,1,0:T(8,128)(2,1)} %bitcast.16), calls=%async_computation | async-start | bytes 1441792 | tf_op jit(solution)/shard_map/all_to_all | solution.py:511
  9.7 22.6 %copy-start = (bf16[5,1280]{1,0:T(8,128)(2,1)S(1)}, bf16[5,1280]{1,0:T(8,128)(2,1)}, u32[]{:S(2)}) copy-start(bf16[5,1280]{1,0:T(8,128)(2,1)} %refs_9_.1) | copy-start | bytes 38404
  29.1 21.2 %all-to-all-start.2 = ((bf16[32,8,1280]{2,1,0:T(8,128)(2,1)}), bf16[32,8,1280]{2,1,0:T(8,128)(2,1)S(1)}, u32[]{:S(2)}, u32[]{:S(2)}) async-start(bf16[32,8,1280]{2,1,0:T(8,128)(2,1)} %bitcast.17), calls=%async_computation.2 | async-start | bytes 1310720 | tf_op jit(solution)/shard_map/all_to_all | solution.py:511
  50.3 22.6 %all-to-all-start.1 = ((bf16[32,8,1280]{2,1,0:T(8,128)(2,1)}), bf16[32,8,1280]{2,1,0:T(8,128)(2,1)S(1)}, u32[]{:S(2)}, u32[]{:S(2)}) async-start(bf16[32,8,1280]{2,1,0:T(8,128)(2,1)} %bitcast.3), calls=%async_computation.1 | async-start | bytes 1310720 | tf_op jit(solution)/shard_map/all_to_all | solution.py:511
